TPU v7x, 32 devices: a whole 2x2x4 slice. The times are simulated.
32 devices in a mesh: role: 2 (over core), grp: 4 (over y, x), dev: 4 (over z).
Axes of the slice: x: 2, y: 2, z: 4, core: 2. Of those that a mesh axis runs over, the one named last changes fastest.
Arguments:
- tokens: bfloat16 [768, 2048], P(('role', 'grp', 'dev')), may hold values from -6 to 6
- norm_gain: float32 [2048], replicated, may hold values from 0.1 to 1.9
- q_gain: float32 [128], replicated, may hold values from 0.1 to 1.9
- k_gain: float32 [128], replicated, may hold values from 0.1 to 1.9
- post_gain: float32 [2048], replicated, may hold values from 0.1 to 1.9
- w_query: bfloat16 [2048, 4096], P(None, 'dev'), may hold values from -0.125 to 0.125
- w_keyvalue: bfloat16 [2048, 1024], P(None, 'dev'), may hold values from -0.125 to 0.125
- w_out: bfloat16 [4096, 2048], P('dev'), may hold values from -0.09375 to 0.09375
- cache_keys: bfloat16 [768, 4, 128, 128], P(('role', 'grp', 'dev')), may hold values from -400 to 400
- cache_values: bfloat16 [768, 4, 128, 128], P(('role', 'grp', 'dev')), may hold values from -6 to 6
- lengths: int32 [768], P(('role', 'grp', 'dev')), may hold values from 1 to 128
- expert_ids: int32 [768, 8], P(('role', 'grp', 'dev')), may hold values from 0 to 15, all different within a row; in each aligned block of 24 rows (0 to 23, 24 to 47, ...) at most 13 rows name the same one
- w_gate: bfloat16 [16, 2048, 768], P(('grp', 'dev'), None, 'role'), may hold values from -0.125 to 0.125
- w_up: bfloat16 [16, 2048, 768], P(('grp', 'dev'), None, 'role'), may hold values from -0.125 to 0.125
- w_down: bfloat16 [16, 768, 2048], P(('grp', 'dev'), 'role'), may hold values from -0.21875 to 0.21875
Outputs:
- layer_out: bfloat16 [768, 2048], P(('role', 'grp', 'dev'))
Inputs may be any that keep to these rules, and one draw needn't show every extreme that they name: `expert_ids`: each row names 8 different experts. Among the 24 rows of one device no expert is named more than 13 times; in the rows of some devices one expert is named exactly 13 times.
All inputs are finite; a program needn't handle non-finite values.
Results may differ from a plain program's by a relative error of at most 0.0099.
Values may be sent and summed in bfloat16 or wider, within the bound.
No kernel may reach another device: no remote copies, remote signals or barrier semaphores. Data moves between devices by JAX's collectives and lax.ppermute only.
A program may use at most 128 MiB of HBM per device.

v0:
```python
import functools

import jax
import jax.numpy as jnp
from jax import lax
from jax.experimental import pallas as pl
from jax.experimental.pallas import tpu as pltpu
from jax.sharding import PartitionSpec as P


epsilon = 1e-06
rope_base = 1000000.0
LANES = 128
VMEM = pl.BlockSpec(memory_space=pltpu.VMEM)
SMEM = pl.BlockSpec(memory_space=pltpu.SMEM)
ANY = pl.BlockSpec(memory_space=pl.ANY)
F32 = jnp.float32
BF16 = jnp.bfloat16


def call(kernel, outs, specs, args, scratch=(), cost=None, limit=None, kept=True):
    flops, moved = cost or (0, 0)
    place = pltpu.VMEM if kept else jax.ShapeDtypeStruct
    return pl.pallas_call(
        kernel,
        out_shape=[place(shape, dtype) for shape, dtype in outs],
        in_specs=list(specs),
        out_specs=[VMEM] * len(outs),
        scratch_shapes=list(scratch),
        cost_estimate=pl.CostEstimate(flops=flops, bytes_accessed=moved, transcendentals=0),
        compiler_params=pltpu.CompilerParams(vmem_limit_bytes=limit),
    )(*args)


def exchange(pieces, axis, size):
    got = [pieces[0]]
    for step in range(1, size):
        got.append(lax.ppermute(pieces[step], axis, [(i, i ^ step) for i in range(size)]))
    return got


def fetch_kernel(count, _, *refs):
    sources, targets, sems = refs[:count], refs[count : 2 * count], refs[2 * count]
    copies = [pltpu.make_async_copy(a, b, sems.at[i]) for i, (a, b) in enumerate(zip(sources, targets))]
    for copy in copies:
        copy.start()
    for copy in copies:
        copy.wait()


def fetch(after, *arrays, held=True):
    moved = sum(a.size * a.dtype.itemsize for a in arrays)
    return call(
        functools.partial(fetch_kernel, len(arrays)),
        [(a.shape, a.dtype) for a in arrays],
        [SMEM] + [ANY] * len(arrays),
        [after] + [pltpu.with_memory_space_constraint(a, pltpu.HBM) if held else a for a in arrays],
        scratch=[pltpu.SemaphoreType.DMA((len(arrays),))],
        cost=(0, moved),
        limit=1 << 20,
    )


def rms(values, gain):
    mean_square = jnp.mean(values * values, axis=-1, keepdims=True)
    return values * lax.rsqrt(mean_square + epsilon) * gain


def stack(refs):
    return jnp.concatenate([ref[...].astype(F32) for ref in refs], axis=0)


def project_kernel(count, *refs):
    blocks, (gain, w_query, w_keyvalue, ids), outs = refs[:count], refs[count : count + 4], refs[count + 4 :]
    rows = blocks[0].shape[0]
    query_width = w_query.shape[1]
    kv_width = w_keyvalue.shape[1]
    normed = rms(stack(blocks), gain[...]).astype(BF16)
    queries = jnp.dot(normed, w_query[...], preferred_element_type=F32)
    fresh = jnp.dot(normed, w_keyvalue[...], preferred_element_type=F32)
    for step in range(count):
        own = slice(step * rows, (step + 1) * rows)
        outs[step][:, :query_width] = queries[own].astype(BF16)
        outs[step][:, query_width : query_width + kv_width] = fresh[own].astype(BF16)
        outs[step][:, query_width + kv_width :] = ids[...]


def turn(values, gain, cosine, sine):
    values = rms(values, gain)
    return values * cosine + pltpu.roll(values, values.shape[1] // 2, 1) * sine


def attend_cache(message, head, gain, cosine, sine, bias, keys, values, scratch):
    rows, _, _, dim = keys.shape
    group = scratch.shape[0] // rows
    for h in range(group):
        piece = message[:, h * dim : (h + 1) * dim].astype(F32)
        scratch[pl.ds(h, rows, stride=group), :] = turn(piece, gain, cosine, sine)
    query = scratch[...].reshape(rows, group, dim).astype(BF16)
    scores = jnp.einsum("rqd,rkd->rqk", query, keys[:, head], preferred_element_type=F32) * dim ** (-0.5)
    scores = scores + bias[:, None, :]
    top = jnp.max(scores, axis=-1, keepdims=True)
    weights = jnp.exp(scores - top)
    total = jnp.sum(weights, axis=-1, keepdims=True)
    mixed = jnp.einsum("rqk,rkd->rqd", weights.astype(BF16), values[:, head], preferred_element_type=F32)
    return query.astype(F32), top, total, mixed


def attend_kernel(steps, me_ref, *refs):
    count = len(steps)
    messages = refs[:count]
    gain, cosine, sine, bias, keys, values = refs[count : count + 6]
    outs, scratch = refs[count + 7 : -1], refs[-1]
    for i, step in enumerate(steps):
        found = attend_cache(
            messages[i], me_ref[0] ^ step, gain[...], cosine[...], sine[...], bias[...], keys, values, scratch.at[i]
        )
        for out, value in zip(outs[4 * i : 4 * i + 4], found):
            out[...] = jnp.broadcast_to(value, out.shape)


def mix_kernel(count, done, me_ref, *refs):
    messages, parts = refs[:count], refs[count : count + 4 * done]
    refs = refs[count + 4 * done :]
    q_gain, k_gain, cosine, sine, bias, keys, values = refs[:7]
    outs = refs[7 : 7 + count]
    scratch, k_rot, v_new, kv_all = refs[7 + count :]
    me = me_ref[0]
    rows, heads, _, dim = keys.shape
    group = scratch.shape[1] // rows
    query_width = group * dim
    kv_width = kv_all.shape[2]
    cos, sin = cosine[...], sine[...]
    last = [
        attend_cache(messages[step], me ^ step, q_gain[...], cos, sin, bias[...], keys, values, scratch.at[step])
        for step in range(done, count)
    ]
    for step in range(count):
        kv_all[me ^ step] = messages[step][:, query_width : query_width + kv_width].astype(F32)
    for h in range(2 * heads):
        column = h * dim
        piece = kv_all[column // kv_width, :, column % kv_width : column % kv_width + dim]
        if h < heads:
            k_rot[h] = turn(piece, k_gain[...], cos, sin).astype(BF16).astype(F32)
        else:
            v_new[h - heads] = piece
    for step in reversed(range(count)):
        head = me ^ step
        if step < done:
            query, top, total, mixed = [ref[...] for ref in parts[4 * step : 4 * step + 4]]
            top, total = top[:, :, :1], total[:, :, :1]
        else:
            query, top, total, mixed = last[step - done]
        new = jnp.sum(query * k_rot[head][:, None, :], axis=-1, keepdims=True) * dim ** (-0.5)
        highest = jnp.maximum(top, new)
        old = jnp.exp(top - highest)
        new = jnp.exp(new - highest)
        share = 1.0 / (total * old + new)
        out = mixed * (old * share) + (new * share) * v_new[head][:, None, :]
        scratch[step] = out.reshape(rows * group, dim)
        for h in range(group):
            outs[step][:, h * dim : (h + 1) * dim] = scratch[step, pl.ds(h, rows, stride=group), :].astype(BF16)


def out_kernel(count, *refs):
    blocks, w_out, outs = refs[:count], refs[count], refs[count + 1 :]
    rows = blocks[0].shape[0]
    partial = jnp.dot(stack(blocks).astype(BF16), w_out[...], preferred_element_type=F32)
    for step in range(count):
        outs[step][...] = partial[step * rows : (step + 1) * rows].astype(outs[step].dtype)


def ready_kernel(count, *refs):
    blocks, (tokens, gain), (hidden, ready) = refs[:count], refs[count : count + 2], refs[count + 2 :]
    total = blocks[0][...]
    for block in blocks[1:]:
        total = total + block[...].astype(F32)
    total = tokens[...].astype(F32) + total
    hidden[...] = total
    ready[...] = rms(total, gain[...]).astype(BF16)


def route_kernel(count, groups, capacity, where_ref, *refs):
    messages, outs = refs[:count], refs[count:]
    dev, grp = where_ref[0], where_ref[1]
    rows, columns = messages[0].shape
    total = count * rows
    lane = lax.broadcasted_iota(jnp.int32, (total, LANES), 1)
    down = lax.broadcasted_iota(jnp.int32, (total, total), 0)
    across = lax.broadcasted_iota(jnp.int32, (total, total), 1)
    earlier = jnp.where((across < down) & (across // rows == down // rows), 1.0, 0.0).astype(BF16)
    table = jnp.concatenate([m[:, columns - LANES :].astype(F32) for m in messages], axis=0)
    named = jnp.zeros((total, LANES), F32)
    for step in range(groups):
        expert = ((grp ^ step) * count + dev).astype(F32)
        hit = jnp.max(jnp.where(table == expert, 1.0, 0.0), axis=1, keepdims=True)
        named = jnp.where(lane == step, hit, named)
    rank = jnp.dot(earlier, named.astype(BF16), preferred_element_type=F32)
    source = (lax.broadcasted_iota(jnp.int32, (total, LANES), 0) // rows).astype(F32)
    slot = rank + source * capacity
    first = 0
    for out in outs:
        held = out.shape[0]
        stride = out.shape[1] // groups
        place = lax.broadcasted_iota(jnp.int32, out.shape, 1).astype(F32)
        chosen = jnp.zeros(out.shape, F32)
        for step in range(groups):
            at = slot[:held, step : step + 1] - first
            inside = (at >= 0) & (at < stride) & (named[:held, step : step + 1] > 0)
            chosen = jnp.where((place == at + step * stride) & inside, 1.0, chosen)
        out[...] = chosen.astype(BF16)
        first += stride


def pack_kernel(count, *refs):
    blocks, choice, outs = refs[:count], refs[count], refs[count + 2 :]
    stride = outs[0].shape[0]
    packed = lax.dot_general(
        choice[...], stack(blocks).astype(BF16), (((0,), (0,)), ((), ())), preferred_element_type=F32
    )
    for step, out in enumerate(outs):
        out[...] = packed[step * stride : (step + 1) * stride].astype(BF16)


def expert_kernel(groups, *refs):
    blocks, weights, outs = refs[:groups], refs[groups : groups + 6], refs[groups + 6 :]
    stride = outs[0].shape[0]
    inputs = stack(blocks).astype(BF16)
    total = None
    for half in range(2):
        gate, up, down = weights[3 * half : 3 * half + 3]
        gated = jnp.dot(inputs, gate[...], preferred_element_type=F32)
        upper = jnp.dot(inputs, up[...], preferred_element_type=F32)
        active = (gated / (1.0 + jnp.exp(-gated)) * upper).astype(BF16)
        part = jnp.dot(active, down[...], preferred_element_type=F32)
        total = part if total is None else total + part
    for step, out in enumerate(outs):
        out[...] = total[step * stride : (step + 1) * stride].astype(BF16)


def combine_kernel(groups, sets, start, *refs):
    choices, outs = refs[sets * groups : sets * (groups + 1)], refs[sets * (groups + 1) + 1 :]
    rows = outs[0].shape[0]
    summed = None
    for i, choice in enumerate(choices):
        part = jnp.dot(
            choice[start : start + len(outs) * rows],
            stack(refs[i * groups : (i + 1) * groups]).astype(BF16),
            preferred_element_type=F32,
        )
        summed = part if summed is None else summed + part
    for step, out in enumerate(outs):
        out[...] = summed[step * rows : (step + 1) * rows].astype(out.dtype)


def final_kernel(count, picks, *refs):
    blocks, hidden, out = refs[:count], refs[count], refs[count + 1]
    total = blocks[0][...]
    for block in blocks[1:]:
        total = total + block[...].astype(F32)
    out[...] = (hidden[...] + total / picks).astype(BF16)


def body(
    tokens,
    norm_gain,
    q_gain,
    k_gain,
    post_gain,
    w_query,
    w_keyvalue,
    w_out,
    cache_keys,
    cache_values,
    lengths,
    expert_ids,
    w_gate,
    w_up,
    w_down,
):
    count, groups = lax.axis_size("dev"), lax.axis_size("grp")
    rows, width = tokens.shape
    picks = expert_ids.shape[1]
    heads, places, dim = cache_keys.shape[1:]
    query_width, kv_width = w_query.shape[1], w_keyvalue.shape[1]
    group = query_width // dim
    experts = count * groups
    capacity = min(rows, max(3, (rows * picks + experts - 1) // experts + 1))
    strides = [max(8, count // 2 * capacity // 8 * 8)]
    strides.append(max(8, -(-(count * capacity - strides[0]) // 8) * 8))
    where = jnp.stack([lax.axis_index("dev"), lax.axis_index("grp")])

    half = count // 2
    near, far = list(range(half)), list(range(half, count))
    swap = [(0, 1), (1, 0)]
    own_weights = [w_gate[0], w_up[0], w_down[0]]
    gathered = exchange([tokens] * count, "dev", count)
    other_weights = [lax.ppermute(w, "role", swap) for w in own_weights]
    query_kept, kv_kept, tokens_kept, gain_kept = fetch(where, w_query, w_keyvalue, tokens, norm_gain.reshape(1, -1))
    gathered[0] = tokens_kept

    ids = jnp.pad(expert_ids.astype(BF16), ((0, 0), (0, LANES - picks)), constant_values=-1)
    frequency = rope_base ** (-jnp.arange(dim // 2, dtype=F32) / (dim // 2))
    angles = lengths.astype(F32)[:, None] * frequency[None, :]
    cosine, sine = jnp.cos(angles), jnp.sin(angles)
    cosine = jnp.concatenate([cosine, cosine], axis=1)
    sine = jnp.concatenate([-sine, sine], axis=1)
    visible = jnp.arange(places, dtype=jnp.int32)[None, :] < lengths[:, None]
    bias = jnp.where(visible, 0.0, -jnp.inf).astype(F32)

    chunks = [near, far]
    messages = [None] * count
    for chunk in chunks:
        made = call(
            functools.partial(project_kernel, len(chunk)),
            [((rows, query_width + kv_width + LANES), BF16)] * len(chunk),
            [VMEM] * (len(chunk) + 4),
            [*[gathered[step] for step in chunk], gain_kept, query_kept, kv_kept, ids],
            cost=(2 * len(chunk) * rows * width * (query_width + kv_width), 3 << 20),
            limit=4 << 20,
        )
        for step, message in zip(chunk, made):
            messages[step] = message
    messages = exchange(messages, "dev", count)
    parts = []
    gains = [q_gain.reshape(1, -1), k_gain.reshape(1, -1)]
    flops = 4 * rows * group * places * dim
    for chunk in chunks[:-1]:
        parts += call(
            functools.partial(attend_kernel, chunk),
            [((rows, group, dim), F32)] * (4 * len(chunk)),
            [SMEM] + [VMEM] * (len(chunk) + 6) + [ANY],
            [where, *[messages[step] for step in chunk], gains[0], cosine, sine, bias]
            + [cache_keys, cache_values, parts[-1] if parts else bias],
            scratch=[pltpu.VMEM((len(chunk), rows * group, dim), F32)],
            cost=(len(chunk) * flops, 2 << 20),
            limit=4 << 20,
        )
    mixtures = call(
        functools.partial(mix_kernel, count, half),
        [((rows, query_width), BF16)] * count,
        [SMEM] + [VMEM] * (count + 4 * half + 7),
        [where, *messages, *parts, *gains, cosine, sine, bias, cache_keys, cache_values],
        scratch=[
            pltpu.VMEM((count, rows * group, dim), F32),
            pltpu.VMEM((heads, rows, dim), F32),
            pltpu.VMEM((heads, rows, dim), F32),
            pltpu.VMEM((count, rows, kv_width), F32),
        ],
        cost=(flops, 2 << 20),
        limit=4 << 20,
    )
    choices = call(
        functools.partial(route_kernel, count, groups, capacity),
        [((half * rows, groups * strides[0]), BF16), ((count * rows, groups * strides[1]), BF16)],
        [SMEM] + [VMEM] * count,
        [where, *messages],
        cost=(0, 2 << 20),
        limit=2 << 20,
    )
    mixtures = exchange(mixtures, "dev", count)
    partials = [None] * count
    for chunk in chunks:
        made = call(
            functools.partial(out_kernel, len(chunk)),
            [((rows, width), BF16 if step else F32) for step in chunk],
            [VMEM] * (len(chunk) + 1),
            [*[mixtures[step] for step in chunk], w_out],
            cost=(2 * len(chunk) * rows * width * query_width, 2 << 20),
            limit=4 << 20,
        )
        for step, partial in zip(chunk, made):
            partials[step] = partial
    partials = exchange(partials, "dev", count)
    hidden, ready = call(
        functools.partial(ready_kernel, count),
        [((rows, width), F32), ((rows, width), BF16)],
        [VMEM] * (count + 2),
        [*partials, tokens_kept, post_gain.reshape(1, -1)],
        cost=(0, 1 << 20),
        limit=8 << 20,
    )
    ready = exchange([ready] * count, "dev", count)
    other_weights = fetch(where, *other_weights, held=False)
    results = []
    after = hidden
    for part, choice, stride in zip((near, near + far), choices, strides):
        packed = call(
            functools.partial(pack_kernel, len(part)),
            [((stride, width), BF16)] * groups,
            [VMEM] * (len(part) + 1) + [ANY],
            [*[ready[step] for step in part], choice, after],
            cost=(0, 1 << 20),
            limit=4 << 20,
        )
        after = packed[0]
        packed = exchange(packed, "grp", groups)
        results.append(
            call(
                functools.partial(expert_kernel, groups),
                [((stride, width), BF16)] * groups,
                [VMEM] * (groups + 6),
                [*packed, *own_weights, *other_weights],
                cost=(6 * groups * stride * width * w_gate.shape[2] * 2, 4 << 20),
                limit=8 << 20,
            )
        )
    results = lax.optimization_barrier(results)
    sums = [None] * count
    after = hidden
    held = [None, exchange(results[1], "grp", groups)]
    held[0] = exchange(results[0], "grp", groups)
    for part, used in ((far, [1]), (near, [0, 1])):
        made = call(
            functools.partial(combine_kernel, groups, len(used), part[0] * rows),
            [((rows, width), BF16 if step else F32) for step in part],
            [VMEM] * (len(used) * (groups + 1)) + [ANY],
            [*sum([held[i] for i in used], []), *[choices[i] for i in used], after],
            cost=(0, 1 << 20),
            limit=4 << 20,
        )
        after = made[0]
        for step, total in zip(part, made):
            sums[step] = total
    sums = exchange(sums, "dev", count)
    [output] = call(
        functools.partial(final_kernel, count, picks),
        [((rows, width), BF16)],
        [VMEM] * (count + 1),
        [*sums, hidden],
        cost=(0, 1 << 20),
        limit=8 << 20,
        kept=False,
    )
    return output


def rms_scale(values, gain):
    widened = values.astype(jnp.float32)
    mean_square = jnp.mean(widened * widened, axis=-1, keepdims=True)
    return widened * lax.rsqrt(mean_square + epsilon) * gain


def rotate(values, positions):
    half_dim = values.shape[-1] // 2
    frequency = rope_base ** (-jnp.arange(half_dim, dtype=jnp.float32) / half_dim)
    angles = positions.astype(jnp.float32)[:, None, None] * frequency[None, None, :]
    cosine = jnp.cos(angles)
    sine_part = jnp.sin(angles)
    first_half = values[..., :half_dim]
    second_half = values[..., half_dim:]
    return jnp.concatenate(
        [
            first_half * cosine - second_half * sine_part,
            second_half * cosine + first_half * sine_part,
        ],
        axis=-1,
    )


def attend(queries, fresh_kv, cache_keys, cache_values, lengths, q_gain, k_gain):
    batch_rows = queries.shape[0]
    kv_heads = cache_keys.shape[1]
    cache_len = cache_keys.shape[2]
    head_dim = cache_keys.shape[3]
    head_count = queries.shape[1] // head_dim
    group_size = head_count // kv_heads
    scaled_q = rotate(
        rms_scale(queries.reshape(batch_rows, head_count, head_dim), q_gain), lengths
    ).astype(jnp.bfloat16)
    fresh_keys = fresh_kv[:, : kv_heads * head_dim].reshape(batch_rows, kv_heads, head_dim)
    fresh_values = fresh_kv[:, kv_heads * head_dim :].reshape(batch_rows, kv_heads, head_dim)
    scaled_k = rotate(rms_scale(fresh_keys, k_gain), lengths).astype(jnp.bfloat16)
    grouped = scaled_q.reshape(batch_rows, kv_heads, group_size, head_dim)
    factor = head_dim ** (-0.5)
    old_scores = (
        jnp.einsum("rgqd,rgkd->rgqk", grouped, cache_keys, preferred_element_type=jnp.float32)
        * factor
    )
    new_scores = (
        jnp.einsum("rgqd,rgd->rgq", grouped, scaled_k, preferred_element_type=jnp.float32) * factor
    )
    visible = jnp.arange(cache_len, dtype=jnp.int32)[None, :] < lengths[:, None]
    old_scores = jnp.where(visible[:, None, None, :], old_scores, -jnp.inf)
    highest = jnp.maximum(jnp.max(old_scores, axis=-1), new_scores)
    old_weights = jnp.exp(old_scores - highest[..., None])
    new_weights = jnp.exp(new_scores - highest)
    denominator = jnp.sum(old_weights, axis=-1) + new_weights
    old_weights = (old_weights / denominator[..., None]).astype(jnp.bfloat16)
    new_weights = (new_weights / denominator).astype(jnp.bfloat16)
    mixture = jnp.einsum(
        "rgqk,rgkd->rgqd", old_weights, cache_values, preferred_element_type=jnp.float32
    )
    mixture = (
        mixture
        + new_weights.astype(jnp.float32)[..., None]
        * fresh_values.astype(jnp.float32)[:, :, None, :]
    )
    return mixture.reshape(batch_rows, head_count * head_dim).astype(jnp.bfloat16)


def expert_rows(inputs, gate_w, up_w, down_w):
    gate_part = jnp.dot(inputs, gate_w, preferred_element_type=jnp.float32)
    upper_part = jnp.dot(inputs, up_w, preferred_element_type=jnp.float32)
    activated = (jax.nn.silu(gate_part) * upper_part).astype(jnp.bfloat16)
    return jnp.dot(activated, down_w, preferred_element_type=jnp.float32)


def general_body(
    tokens,
    norm_gain,
    q_gain,
    k_gain,
    post_gain,
    w_query,
    w_keyvalue,
    w_out,
    cache_keys,
    cache_values,
    lengths,
    expert_ids,
    w_gate,
    w_up,
    w_down,
):
    normed = rms_scale(tokens, norm_gain).astype(jnp.bfloat16)
    query_width = w_query.shape[1]
    piece = lax.all_gather(normed, "dev", axis=0, tiled=True)
    joined = jnp.concatenate(
        [
            jnp.dot(piece, w_query, preferred_element_type=jnp.float32),
            jnp.dot(piece, w_keyvalue, preferred_element_type=jnp.float32),
        ],
        axis=1,
    )
    projected = joined.astype(jnp.bfloat16)
    queries, fresh_kv = (
        lax.all_to_all(projected[:, :query_width], "dev", split_axis=0, concat_axis=1, tiled=True),
        lax.all_to_all(projected[:, query_width:], "dev", split_axis=0, concat_axis=1, tiled=True),
    )
    mixture = attend(queries, fresh_kv, cache_keys, cache_values, lengths, q_gain, k_gain)
    head_rows = lax.all_to_all(mixture, "dev", split_axis=1, concat_axis=0, tiled=True)
    own_rows = tokens.shape[0]
    attended = lax.psum_scatter(
        jnp.dot(head_rows, w_out, preferred_element_type=jnp.float32).astype(jnp.bfloat16),
        "dev",
        scatter_dimension=0,
        tiled=True,
    ).astype(jnp.float32)
    hidden = tokens.astype(jnp.float32) + attended
    ready = rms_scale(hidden, post_gain).astype(jnp.bfloat16)
    picks = expert_ids.shape[1]
    group_count = lax.axis_size("grp")
    member_count = lax.axis_size("dev")
    expert_count = group_count * member_count
    capacity = min(own_rows, max(3, (own_rows * picks + expert_count - 1) // expert_count + 1))
    model_width = tokens.shape[1]
    flat_ids = expert_ids.reshape(own_rows * picks)
    order_index = jnp.arange(own_rows * picks, dtype=jnp.int32)
    earlier = (flat_ids[:, None] == flat_ids[None, :]) & (
        order_index[None, :] < order_index[:, None]
    )
    slot_index = jnp.sum(earlier.astype(jnp.int32), axis=1)
    position = (flat_ids * capacity + slot_index).reshape(own_rows, picks)
    buffer_rows = jnp.arange(expert_count * capacity, dtype=jnp.int32)
    placing = jnp.any(position[None, :, :] == buffer_rows[:, None, None], axis=2).astype(
        jnp.bfloat16
    )
    outgoing = jnp.dot(placing, ready, preferred_element_type=jnp.float32).astype(jnp.bfloat16)
    arrived = lax.all_to_all(
        outgoing.reshape(expert_count, capacity, model_width),
        ("grp", "dev"),
        split_axis=0,
        concat_axis=0,
        tiled=True,
    )
    arrived = arrived.reshape(expert_count * capacity, model_width)
    full_gate, full_up, full_down = (
        lax.all_gather(w_gate, "role", axis=2, tiled=True),
        lax.all_gather(w_up, "role", axis=2, tiled=True),
        lax.all_gather(w_down, "role", axis=1, tiled=True),
    )
    expert_out = expert_rows(arrived, full_gate[0], full_up[0], full_down[0]).astype(jnp.bfloat16)
    returned = lax.all_to_all(
        expert_out.reshape(expert_count, capacity, model_width),
        ("grp", "dev"),
        split_axis=0,
        concat_axis=0,
        tiled=True,
    )
    returned = returned.reshape(expert_count * capacity, model_width)
    selected = (
        jnp.take(returned, position.reshape(own_rows * picks), axis=0)
        .astype(jnp.float32)
        .reshape(own_rows, picks, model_width)
    )
    output = hidden + jnp.sum(selected, axis=1) / picks
    return output.astype(jnp.bfloat16)


def solution(mesh):
    sizes = dict(mesh.shape)

    def step(*args):
        heads = args[8].shape[1]
        powers = all(sizes[axis] & (sizes[axis] - 1) == 0 for axis in ("grp", "dev"))
        fitted = sizes["dev"] == heads and sizes["role"] == 2 and powers
        if not fitted:
            return general_body(*args)
        return body(*args)

    return jax.shard_map(
        step,
        mesh=mesh,
        in_specs=(
            P(("role", "grp", "dev"), None),
            P(),
            P(),
            P(),
            P(),
            P(None, "dev"),
            P(None, "dev"),
            P("dev", None),
            P(("role", "grp", "dev"), None, None, None),
            P(("role", "grp", "dev"), None, None, None),
            P(("role", "grp", "dev")),
            P(("role", "grp", "dev"), None),
            P(("grp", "dev"), None, "role"),
            P(("grp", "dev"), None, "role"),
            P(("grp", "dev"), "role", None),
        ),
        out_specs=P(("role", "grp", "dev"), None),
        check_vma=False,
    )
```

profile of v0, /device:TPU:0, one launch (start us, length us, event | category | flops | bytes accessed | tf_op | source)
XLA Modules:
  0.0 99.7 jit_solution(10279150774130230939)
XLA Ops:
  1.0 2.6 %collective-permute-start = (bf16[24,2048]{1,0:T(8,128)(2,1)}, bf16[24,2048]{1,0:T(8,128)(2,1)S(1)}, u32[]{:S(2)}, u32[]{:S(2)}) collective-permute-start(bf16[24,2048]{1,0:T(8,128)(2,1)} %refs_2_.3), channel_id=1, source_target_pairs={{0,1},{1,0},{2,3},{3,2},{4,5},{5,4},{6,7},{7,6},{8,9},{9,8},{10,11... | collective-permute-start | bytes 294920 | tf_op jit(solution)/shard_map/ppermute | solution.py:38
  3.6 2.6 %collective-permute-start.2 = (bf16[24,2048]{1,0:T(8,128)(2,1)}, bf16[24,2048]{1,0:T(8,128)(2,1)S(1)}, u32[]{:S(2)}, u32[]{:S(2)}) collective-permute-start(bf16[24,2048]{1,0:T(8,128)(2,1)} %refs_2_.3), channel_id=1, source_target_pairs={{0,2},{1,3},{2,0},{3,1},{4,6},{5,7},{6,4},{7,5},{8,10},{9,11},{10,... | collective-permute-start | bytes 294920 | tf_op jit(solution)/shard_map/ppermute | solution.py:38
  7.8 3.1 %shard_map.145 = (bf16[2048,1024]{1,0:T(8,128)(2,1)S(1)}, bf16[2048,256]{1,0:T(8,128)(2,1)S(1)}, bf16[24,2048]{1,0:T(8,128)(2,1)S(1)}, f32[1,2048]{1,0:T(1,128)S(1)}) custom-call(s32[2]{0:T(128)S(1)} %pad_add_fusion._.me_ref.where_ref, bf16[2048,1024]{1,0:T(8,128)(2,1)} %refs_0_.1, bf16[2048,256]{1,0:T(8,128)(2,1)} %refs_1_.1, bf16[24,2048]{1,0:T(8,128)(2,1)} %refs_2_.3, ...), custom_call_target="tpu_custom_call" | custom-call | bytes 5349376 | tf_op jit(solution)/shard_map/pallas_call | solution.py:24
  13.4 4.8 %collective-permute-done.3.refs_1_ = bf16[24,2048]{1,0:T(8,128)(2,1)S(1)} collective-permute-done((bf16[24,2048]{1,0:T(8,128)(2,1)S(1)}, bf16[24,2048]{1,0:T(8,128)(2,1)S(1)}, u32[]{:S(2)}, u32[]{:S(2)}) %collective-permute-start.3) | collective-permute-done | bytes 98336 | tf_op jit(solution)/shard_map/ppermute | solution.py:38
  21.1 2.0 %shard_map.148 = (f32[24,8,128]{2,1,0:T(8,128)S(1)}, f32[24,8,128]{2,1,0:T(8,128)S(1)}, f32[24,8,128]{2,1,0:T(8,128)S(1)}, f32[24,8,128]{2,1,0:T(8,128)S(1)}, f3...) custom-call(s32[2]{0:T(128)S(1)} %pad_add_fusion._.me_ref.where_ref,, ...), custom_call_target="tpu_custom_call" | custom-call | flops 25165824 | bytes 2097152 | tf_op jit(solution)/shard_map/pallas_call | solution.py:24
  23.1 1.8 %collective-permute-done.4.refs_2_ = bf16[24,1408]{1,0:T(8,128)(2,1)S(1)} collective-permute-done((bf16[24,1408]{1,0:T(8,128)(2,1)S(1)}, bf16[24,1408]{1,0:T(8,128)(2,1)S(1)}, u32[]{:S(2)}, u32[]{:S(2)}) %collective-permute-start.4) | collective-permute-done | bytes 67616 | tf_op jit(solution)/shard_map/ppermute | solution.py:38
  25.7 3.2 %shard_map.149 = (bf16[24,1024]{1,0:T(8,128)(2,1)S(1)}, bf16[24,1024]{1,0:T(8,128)(2,1)S(1)}, bf16[24,1024]{1,0:T(8,128)(2,1)S(1)}, bf16[24,1024]{1,0:T(8,128)(2,1)S(1)}) custom-call(s32[2]{0:T(128)S(1)} %pad_add_fusion._.me_ref.where_ref, bf16[24,1408]{1,0:T(8,128)(2,1)S(1)} %get-tuple-element.68.refs_0_, ...), custom_call_target="tpu_custom_call" | custom-call | flops 12582912 | bytes 2097152 | tf_op jit(solution)/shard_map/pallas_call | solution.py:24
  31.4 1.6 %collective-permute-done.6.refs_1_ = bf16[24,1024]{1,0:T(8,128)(2,1)S(1)} collective-permute-done((bf16[24,1024]{1,0:T(8,128)(2,1)S(1)}, bf16[24,1024]{1,0:T(8,128)(2,1)S(1)}, u32[]{:S(2)}, u32[]{:S(2)}) %collective-permute-start.6) | collective-permute-done | bytes 49184 | tf_op jit(solution)/shard_map/ppermute | solution.py:38
  36.0 1.9 %collective-permute-start.9 = (bf16[24,1024]{1,0:T(8,128)(2,1)S(1)}, bf16[24,1024]{1,0:T(8,128)(2,1)S(1)}, u32[]{:S(2)}, u32[]{:S(2)}) collective-permute-start(bf16[24,1024]{1,0:T(8,128)(2,1)S(1)} %get-tuple-element.85), channel_id=1, source_target_pairs={{0,3},{1,2},{2,1},{3,0},{4,7},{5,6},{6,5},{7,4},{8,11},{9,10},{10,... | collective-permute-start | bytes 147464 | tf_op jit(solution)/shard_map/ppermute | solution.py:38
  37.9 4.6 %collective-permute-done.9.refs_1_ = bf16[24,1024]{1,0:T(8,128)(2,1)S(1)} collective-permute-done((bf16[24,1024]{1,0:T(8,128)(2,1)S(1)}, bf16[24,1024]{1,0:T(8,128)(2,1)S(1)}, u32[]{:S(2)}, u32[]{:S(2)}) %collective-permute-start.9) | collective-permute-done | bytes 49184 | tf_op jit(solution)/shard_map/ppermute | solution.py:38
  44.9 4.1 %collective-permute-done.10.refs_2_ = bf16[24,2048]{1,0:T(8,128)(2,1)S(1)} collective-permute-done((bf16[24,2048]{1,0:T(8,128)(2,1)S(1)}, bf16[24,2048]{1,0:T(8,128)(2,1)S(1)}, u32[]{:S(2)}, u32[]{:S(2)}) %collective-permute-start.10) | collective-permute-done | bytes 98336 | tf_op jit(solution)/shard_map/ppermute | solution.py:38
  49.0 1.9 %collective-permute-done.11.refs_3_ = bf16[24,2048]{1,0:T(8,128)(2,1)S(1)} collective-permute-done((bf16[24,2048]{1,0:T(8,128)(2,1)S(1)}, bf16[24,2048]{1,0:T(8,128)(2,1)S(1)}, u32[]{:S(2)}, u32[]{:S(2)}) %collective-permute-start.11) | collective-permute-done | bytes 98336 | tf_op jit(solution)/shard_map/ppermute | solution.py:38
  51.2 2.5 %collective-permute-start.12 = (bf16[24,2048]{1,0:T(8,128)(2,1)S(1)}, bf16[24,2048]{1,0:T(8,128)(2,1)S(1)}, u32[]{:S(2)}, u32[]{:S(2)}) collective-permute-start(bf16[24,2048]{1,0:T(8,128)(2,1)S(1)} %get-tuple-element.88.refs_0_), channel_id=1, source_target_pairs={{0,1},{1,0},{2,3},{3,2},{4,5},{5,4},{6,7},{7,6},{8,9},{9,8},{10,11... | collective-permute-start | bytes 294920 | tf_op jit(solution)/shard_map/ppermute | solution.py:38
  53.7 2.5 %collective-permute-start.19 = (bf16[24,2048]{1,0:T(8,128)(2,1)S(1)}, bf16[24,2048]{1,0:T(8,128)(2,1)S(1)}, u32[]{:S(2)}, u32[]{:S(2)}) collective-permute-start(bf16[24,2048]{1,0:T(8,128)(2,1)S(1)} %get-tuple-element.88.refs_0_), channel_id=1, source_target_pairs={{0,2},{1,3},{2,0},{3,1},{4,6},{5,7},{6,4},{7,5},{8,10},{9,11},{10,... | collective-permute-start | bytes 294920 | tf_op jit(solution)/shard_map/ppermute | solution.py:38
  57.2 2.9 %collective-permute-start.20 = (bf16[24,2048]{1,0:T(8,128)(2,1)S(1)}, bf16[24,2048]{1,0:T(8,128)(2,1)S(1)}, u32[]{:S(2)}, u32[]{:S(2)}) collective-permute-start(bf16[24,2048]{1,0:T(8,128)(2,1)S(1)} %get-tuple-element.88.refs_0_), channel_id=1, source_target_pairs={{0,3},{1,2},{2,1},{3,0},{4,7},{5,6},{6,5},{7,4},{8,11},{9,10},{10,... | collective-permute-start | bytes 294920 | tf_op jit(solution)/shard_map/ppermute | solution.py:38
  62.0 1.8 %collective-permute-done.20.refs_3_ = bf16[24,2048]{1,0:T(8,128)(2,1)S(1)} collective-permute-done((bf16[24,2048]{1,0:T(8,128)(2,1)S(1)}, bf16[24,2048]{1,0:T(8,128)(2,1)S(1)}, u32[]{:S(2)}, u32[]{:S(2)}) %collective-permute-start.20) | collective-permute-done | bytes 98336 | tf_op jit(solution)/shard_map/ppermute | solution.py:38
  65.9 1.9 %collective-permute-start.15 = (bf16[24,2048]{1,0:T(8,128)(2,1)S(1)}, bf16[24,2048]{1,0:T(8,128)(2,1)S(1)}, u32[]{:S(2)}, u32[]{:S(2)}) collective-permute-start(bf16[24,2048]{1,0:T(8,128)(2,1)S(1)} %get-tuple-element.94), channel_id=1, source_target_pairs={{0,12},{4,8},{8,4},{12,0},{1,13},{5,9},{9,5},{13,1},{2,14},{6,10},... | collective-permute-start | bytes 294920 | tf_op jit(solution)/shard_map/ppermute | solution.py:38
  69.8 1.9 %collective-permute-start.23 = (bf16[32,2048]{1,0:T(8,128)(2,1)S(1)}, bf16[32,2048]{1,0:T(8,128)(2,1)S(1)}, u32[]{:S(2)}, u32[]{:S(2)}) collective-permute-start(bf16[32,2048]{1,0:T(8,128)(2,1)S(1)} %get-tuple-element.106), channel_id=1, source_target_pairs={{0,12},{4,8},{8,4},{12,0},{1,13},{5,9},{9,5},{13,1},{2,14},{6,10},... | collective-permute-start | bytes 393224 | tf_op jit(solution)/shard_map/ppermute | solution.py:38
  71.8 2.4 %shard_map.155 = (bf16[2048,384]{1,0:T(8,128)(2,1)S(1)}, bf16[2048,384]{1,0:T(8,128)(2,1)S(1)}, bf16[384,2048]{1,0:T(8,128)(2,1)S(1)}) custom-call(s32[2]{0:T(128)S(1)} %pad_add_fusion._.me_ref.where_ref, bf16[2048,384]{1,0:T(8,128)(2,1)S(1)} %collective-permute-done.16.refs_0_, bf16[2048,384]{1,0:T(8,128)(2,1)S(1)} %collective-permute-done.17.refs_1_, ...), custom_call_target="tpu_custom_call" | custom-call | bytes 4718592 | tf_op jit(solution)/shard_map/pallas_call | solution.py:24
  74.2 1.8 %shard_map.156 = (bf16[24,2048]{1,0:T(8,128)(2,1)S(1)}, bf16[24,2048]{1,0:T(8,128)(2,1)S(1)}, bf16[24,2048]{1,0:T(8,128)(2,1)S(1)}, bf16[24,2048]{1,0:T(8,128)(2,1)S(1)}) custom-call(bf16[24,2048]{1,0:T(8,128)(2,1)S(1)} %get-tuple-element.91.refs_0_.refs_5_, bf16[24,2048]{1,0:T(8,128)(2,1)S(1)} %collective-permute-done.13.refs_1_, ...), custom_call_target="tpu_custom_call" | custom-call | flops 905969664 | bytes 4194304 | tf_op jit(solution)/shard_map/pallas_call | solution.py:24
  77.9 1.9 %shard_map.158 = (bf16[32,2048]{1,0:T(8,128)(2,1)S(1)}, bf16[32,2048]{1,0:T(8,128)(2,1)S(1)}, bf16[32,2048]{1,0:T(8,128)(2,1)S(1)}, bf16[32,2048]{1,0:T(8,128)(2,1)S(1)}) custom-call(bf16[32,2048]{1,0:T(8,128)(2,1)S(1)} %get-tuple-element.103.refs_0_, bf16[32,2048]{1,0:T(8,128)(2,1)S(1)} %collective-permute-done.21.refs_1_, ...), custom_call_target="tpu_custom_call" | custom-call | flops 1207959552 | bytes 4194304 | tf_op jit(solution)/shard_map/pallas_call | solution.py:24
  88.6 2.2 %collective-permute-start.31 = (bf16[24,2048]{1,0:T(8,128)(2,1)S(1)}, bf16[24,2048]{1,0:T(8,128)(2,1)S(1)}, u32[]{:S(2)}, u32[]{:S(2)}) collective-permute-start(bf16[24,2048]{1,0:T(8,128)(2,1)S(1)} %get-tuple-element.119.refs_10_), channel_id=1, source_target_pairs={{0,2},{1,3},{2,0},{3,1},{4,6},{5,7},{6,4},{7,5},{8,10},{9,11},{10,... | collective-permute-start | bytes 294920 | tf_op jit(solution)/shard_map/ppermute | solution.py:38
  92.6 2.7 %collective-permute-start.32 = (bf16[24,2048]{1,0:T(8,128)(2,1)S(1)}, bf16[24,2048]{1,0:T(8,128)(2,1)S(1)}, u32[]{:S(2)}, u32[]{:S(2)}) collective-permute-start(bf16[24,2048]{1,0:T(8,128)(2,1)S(1)} %get-tuple-element.122), channel_id=1, source_target_pairs={{0,3},{1,2},{2,1},{3,0},{4,7},{5,6},{6,5},{7,4},{8,11},{9,10},{10,... | collective-permute-start | bytes 294920 | tf_op jit(solution)/shard_map/ppermute | solution.py:38
  96.4 2.6 %collective-permute-done.32.refs_3_ = bf16[24,2048]{1,0:T(8,128)(2,1)S(1)} collective-permute-done((bf16[24,2048]{1,0:T(8,128)(2,1)S(1)}, bf16[24,2048]{1,0:T(8,128)(2,1)S(1)}, u32[]{:S(2)}, u32[]{:S(2)}) %collective-permute-start.32) | collective-permute-done | bytes 98336 | tf_op jit(solution)/shard_map/ppermute | solution.py:38
  (90 shorter events, 38.0 us)
Async XLA Ops:
  0.0 68.1 %collective-permute-start.16 = (bf16[2048,384]{1,0:T(8,128)(2,1)}, bf16[2048,384]{1,0:T(8,128)(2,1)S(1)}, u32[]{:S(2)}, u32[]{:S(2)}) collective-permute-start(bf16[2048,384]{1,0:T(8,128)(2,1)} %bitcast.9), channel_id=1, source_target_pairs={{0,16},{16,0},{1,17},{17,1},{2,18},{18,2},{3,19},{19,3},{4,20},{20... | collective-permute-start | bytes 4718600 | tf_op jit(solution)/shard_map/ppermute | solution.py:298
  0.5 68.2 %collective-permute-start.17 = (bf16[2048,384]{1,0:T(8,128)(2,1)}, bf16[2048,384]{1,0:T(8,128)(2,1)S(1)}, u32[]{:S(2)}, u32[]{:S(2)}) collective-permute-start(bf16[2048,384]{1,0:T(8,128)(2,1)} %bitcast.12), channel_id=1, source_target_pairs={{0,16},{16,0},{1,17},{17,1},{2,18},{18,2},{3,19},{19,3},{4,20},{20... | collective-permute-start | bytes 4718600 | tf_op jit(solution)/shard_map/ppermute | solution.py:298
  0.5 69.3 %collective-permute-start.18 = (bf16[384,2048]{1,0:T(8,128)(2,1)}, bf16[384,2048]{1,0:T(8,128)(2,1)}, u32[]{:S(2)}, u32[]{:S(2)}) collective-permute-start(bf16[384,2048]{1,0:T(8,128)(2,1)} %bitcast.15), channel_id=1, source_target_pairs={{0,16},{16,0},{1,17},{17,1},{2,18},{18,2},{3,19},{19,3},{4,20},{20... | collective-permute-start | bytes 4718600 | tf_op jit(solution)/shard_map/ppermute | solution.py:298
  1.0 9.9 %collective-permute-start = (bf16[24,2048]{1,0:T(8,128)(2,1)}, bf16[24,2048]{1,0:T(8,128)(2,1)S(1)}, u32[]{:S(2)}, u32[]{:S(2)}) collective-permute-start(bf16[24,2048]{1,0:T(8,128)(2,1)} %refs_2_.3), channel_id=1, source_target_pairs={{0,1},{1,0},{2,3},{3,2},{4,5},{5,4},{6,7},{7,6},{8,9},{9,8},{10,11... | collective-permute-start | bytes 294920 | tf_op jit(solution)/shard_map/ppermute | solution.py:38
  3.6 9.7 %collective-permute-start.2 = (bf16[24,2048]{1,0:T(8,128)(2,1)}, bf16[24,2048]{1,0:T(8,128)(2,1)S(1)}, u32[]{:S(2)}, u32[]{:S(2)}) collective-permute-start(bf16[24,2048]{1,0:T(8,128)(2,1)} %refs_2_.3), channel_id=1, source_target_pairs={{0,2},{1,3},{2,0},{3,1},{4,6},{5,7},{6,4},{7,5},{8,10},{9,11},{10,... | collective-permute-start | bytes 294920 | tf_op jit(solution)/shard_map/ppermute | solution.py:38
  10.9 7.3 %collective-permute-start.3 = (bf16[24,2048]{1,0:T(8,128)(2,1)S(1)}, bf16[24,2048]{1,0:T(8,128)(2,1)S(1)}, u32[]{:S(2)}, u32[]{:S(2)}) collective-permute-start(bf16[24,2048]{1,0:T(8,128)(2,1)S(1)} %copy-done.9), channel_id=1, source_target_pairs={{0,3},{1,2},{2,1},{3,0},{4,7},{5,6},{6,5},{7,4},{8,11},{9,10},{10,... | collective-permute-start | bytes 294920 | tf_op jit(solution)/shard_map/ppermute | solution.py:38
  13.2 6.2 %collective-permute-start.1 = (bf16[24,1408]{1,0:T(8,128)(2,1)S(1)}, bf16[24,1408]{1,0:T(8,128)(2,1)S(1)}, u32[]{:S(2)}, u32[]{:S(2)}) collective-permute-start(bf16[24,1408]{1,0:T(8,128)(2,1)S(1)} %get-tuple-element.69), channel_id=1, source_target_pairs={{0,1},{1,0},{2,3},{3,2},{4,5},{5,4},{6,7},{7,6},{8,9},{9,8},{10,11... | collective-permute-start | bytes 202760 | tf_op jit(solution)/shard_map/ppermute | solution.py:38
  19.4 6.3 %collective-permute-start.5 = (bf16[24,1408]{1,0:T(8,128)(2,1)S(1)}, bf16[24,1408]{1,0:T(8,128)(2,1)S(1)}, u32[]{:S(2)}, u32[]{:S(2)}) collective-permute-start(bf16[24,1408]{1,0:T(8,128)(2,1)S(1)} %get-tuple-element.71), channel_id=1, source_target_pairs={{0,3},{1,2},{2,1},{3,0},{4,7},{5,6},{6,5},{7,4},{8,11},{9,10},{10,... | collective-permute-start | bytes 202760 | tf_op jit(solution)/shard_map/ppermute | solution.py:38
  33.9 9.6 %collective-permute-start.7 = (bf16[24,2048]{1,0:T(8,128)(2,1)S(1)}, bf16[24,2048]{1,0:T(8,128)(2,1)S(1)}, u32[]{:S(2)}, u32[]{:S(2)}) collective-permute-start(bf16[24,2048]{1,0:T(8,128)(2,1)S(1)} %get-tuple-element.83), channel_id=1, source_target_pairs={{0,1},{1,0},{2,3},{3,2},{4,5},{5,4},{6,7},{7,6},{8,9},{9,8},{10,11... | collective-permute-start | bytes 294920 | tf_op jit(solution)/shard_map/ppermute | solution.py:38
  36.0 6.5 %collective-permute-start.9 = (bf16[24,1024]{1,0:T(8,128)(2,1)S(1)}, bf16[24,1024]{1,0:T(8,128)(2,1)S(1)}, u32[]{:S(2)}, u32[]{:S(2)}) collective-permute-start(bf16[24,1024]{1,0:T(8,128)(2,1)S(1)} %get-tuple-element.85), channel_id=1, source_target_pairs={{0,3},{1,2},{2,1},{3,0},{4,7},{5,6},{6,5},{7,4},{8,11},{9,10},{10,... | collective-permute-start | bytes 147464 | tf_op jit(solution)/shard_map/ppermute | solution.py:38
  43.5 7.5 %collective-permute-start.11 = (bf16[24,2048]{1,0:T(8,128)(2,1)S(1)}, bf16[24,2048]{1,0:T(8,128)(2,1)S(1)}, u32[]{:S(2)}, u32[]{:S(2)}) collective-permute-start(bf16[24,2048]{1,0:T(8,128)(2,1)S(1)} %get-tuple-element.87), channel_id=1, source_target_pairs={{0,3},{1,2},{2,1},{3,0},{4,7},{5,6},{6,5},{7,4},{8,11},{9,10},{10,... | collective-permute-start | bytes 294920 | tf_op jit(solution)/shard_map/ppermute | solution.py:38
  51.2 6.1 %collective-permute-start.12 = (bf16[24,2048]{1,0:T(8,128)(2,1)S(1)}, bf16[24,2048]{1,0:T(8,128)(2,1)S(1)}, u32[]{:S(2)}, u32[]{:S(2)}) collective-permute-start(bf16[24,2048]{1,0:T(8,128)(2,1)S(1)} %get-tuple-element.88.refs_0_), channel_id=1, source_target_pairs={{0,1},{1,0},{2,3},{3,2},{4,5},{5,4},{6,7},{7,6},{8,9},{9,8},{10,11... | collective-permute-start | bytes 294920 | tf_op jit(solution)/shard_map/ppermute | solution.py:38
  53.7 6.8 %collective-permute-start.19 = (bf16[24,2048]{1,0:T(8,128)(2,1)S(1)}, bf16[24,2048]{1,0:T(8,128)(2,1)S(1)}, u32[]{:S(2)}, u32[]{:S(2)}) collective-permute-start(bf16[24,2048]{1,0:T(8,128)(2,1)S(1)} %get-tuple-element.88.refs_0_), channel_id=1, source_target_pairs={{0,2},{1,3},{2,0},{3,1},{4,6},{5,7},{6,4},{7,5},{8,10},{9,11},{10,... | collective-permute-start | bytes 294920 | tf_op jit(solution)/shard_map/ppermute | solution.py:38
  57.2 6.6 %collective-permute-start.20 = (bf16[24,2048]{1,0:T(8,128)(2,1)S(1)}, bf16[24,2048]{1,0:T(8,128)(2,1)S(1)}, u32[]{:S(2)}, u32[]{:S(2)}) collective-permute-start(bf16[24,2048]{1,0:T(8,128)(2,1)S(1)} %get-tuple-element.88.refs_0_), channel_id=1, source_target_pairs={{0,3},{1,2},{2,1},{3,0},{4,7},{5,6},{6,5},{7,4},{8,11},{9,10},{10,... | collective-permute-start | bytes 294920 | tf_op jit(solution)/shard_map/ppermute | solution.py:38
  63.8 10.3 %collective-permute-start.14 = (bf16[24,2048]{1,0:T(8,128)(2,1)S(1)}, bf16[24,2048]{1,0:T(8,128)(2,1)S(1)}, u32[]{:S(2)}, u32[]{:S(2)}) collective-permute-start(bf16[24,2048]{1,0:T(8,128)(2,1)S(1)} %get-tuple-element.93), channel_id=1, source_target_pairs={{0,8},{4,12},{8,0},{12,4},{1,9},{5,13},{9,1},{13,5},{2,10},{6,14},... | collective-permute-start | bytes 294920 | tf_op jit(solution)/shard_map/ppermute | solution.py:38
  65.9 8.2 %collective-permute-start.15 = (bf16[24,2048]{1,0:T(8,128)(2,1)S(1)}, bf16[24,2048]{1,0:T(8,128)(2,1)S(1)}, u32[]{:S(2)}, u32[]{:S(2)}) collective-permute-start(bf16[24,2048]{1,0:T(8,128)(2,1)S(1)} %get-tuple-element.94), channel_id=1, source_target_pairs={{0,12},{4,8},{8,4},{12,0},{1,13},{5,9},{9,5},{13,1},{2,14},{6,10},... | collective-permute-start | bytes 294920 | tf_op jit(solution)/shard_map/ppermute | solution.py:38
  68.1 7.9 %collective-permute-start.21 = (bf16[32,2048]{1,0:T(8,128)(2,1)S(1)}, bf16[32,2048]{1,0:T(8,128)(2,1)S(1)}, u32[]{:S(2)}, u32[]{:S(2)}) collective-permute-start(bf16[32,2048]{1,0:T(8,128)(2,1)S(1)} %get-tuple-element.104), channel_id=1, source_target_pairs={{0,4},{4,0},{8,12},{12,8},{1,5},{5,1},{9,13},{13,9},{2,6},{6,2},{1... | collective-permute-start | bytes 393224 | tf_op jit(solution)/shard_map/ppermute | solution.py:38
  68.7 8.7 %collective-permute-start.22 = (bf16[32,2048]{1,0:T(8,128)(2,1)S(1)}, bf16[32,2048]{1,0:T(8,128)(2,1)S(1)}, u32[]{:S(2)}, u32[]{:S(2)}) collective-permute-start(bf16[32,2048]{1,0:T(8,128)(2,1)S(1)} %get-tuple-element.105), channel_id=1, source_target_pairs={{0,8},{4,12},{8,0},{12,4},{1,9},{5,13},{9,1},{13,5},{2,10},{6,14},... | collective-permute-start | bytes 393224 | tf_op jit(solution)/shard_map/ppermute | solution.py:38
  69.8 8.1 %collective-permute-start.23 = (bf16[32,2048]{1,0:T(8,128)(2,1)S(1)}, bf16[32,2048]{1,0:T(8,128)(2,1)S(1)}, u32[]{:S(2)}, u32[]{:S(2)}) collective-permute-start(bf16[32,2048]{1,0:T(8,128)(2,1)S(1)} %get-tuple-element.106), channel_id=1, source_target_pairs={{0,12},{4,8},{8,4},{12,0},{1,13},{5,9},{9,5},{13,1},{2,14},{6,10},... | collective-permute-start | bytes 393224 | tf_op jit(solution)/shard_map/ppermute | solution.py:38
  79.8 6.1 %collective-permute-start.27 = (bf16[32,2048]{1,0:T(8,128)(2,1)S(1)}, bf16[32,2048]{1,0:T(8,128)(2,1)S(1)}, u32[]{:S(2)}, u32[]{:S(2)}) collective-permute-start(bf16[32,2048]{1,0:T(8,128)(2,1)S(1)} %get-tuple-element.116), channel_id=1, source_target_pairs={{0,4},{4,0},{8,12},{12,8},{1,5},{5,1},{9,13},{13,9},{2,6},{6,2},{1... | collective-permute-start | bytes 393224 | tf_op jit(solution)/shard_map/ppermute | solution.py:38
  83.4 7.3 %collective-permute-start.24 = (bf16[24,2048]{1,0:T(8,128)(2,1)S(1)}, bf16[24,2048]{1,0:T(8,128)(2,1)S(1)}, u32[]{:S(2)}, u32[]{:S(2)}) collective-permute-start(bf16[24,2048]{1,0:T(8,128)(2,1)S(1)} %get-tuple-element.112), channel_id=1, source_target_pairs={{0,4},{4,0},{8,12},{12,8},{1,5},{5,1},{9,13},{13,9},{2,6},{6,2},{1... | collective-permute-start | bytes 294920 | tf_op jit(solution)/shard_map/ppermute | solution.py:38
  84.6 6.1 %collective-permute-start.25 = (bf16[24,2048]{1,0:T(8,128)(2,1)S(1)}, bf16[24,2048]{1,0:T(8,128)(2,1)S(1)}, u32[]{:S(2)}, u32[]{:S(2)}) collective-permute-start(bf16[24,2048]{1,0:T(8,128)(2,1)S(1)} %get-tuple-element.113), channel_id=1, source_target_pairs={{0,8},{4,12},{8,0},{12,4},{1,9},{5,13},{9,1},{13,5},{2,10},{6,14},... | collective-permute-start | bytes 294920 | tf_op jit(solution)/shard_map/ppermute | solution.py:38
  88.6 7.9 %collective-permute-start.31 = (bf16[24,2048]{1,0:T(8,128)(2,1)S(1)}, bf16[24,2048]{1,0:T(8,128)(2,1)S(1)}, u32[]{:S(2)}, u32[]{:S(2)}) collective-permute-start(bf16[24,2048]{1,0:T(8,128)(2,1)S(1)} %get-tuple-element.119.refs_10_), channel_id=1, source_target_pairs={{0,2},{1,3},{2,0},{3,1},{4,6},{5,7},{6,4},{7,5},{8,10},{9,11},{10,... | collective-permute-start | bytes 294920 | tf_op jit(solution)/shard_map/ppermute | solution.py:38
  92.6 6.4 %collective-permute-start.32 = (bf16[24,2048]{1,0:T(8,128)(2,1)S(1)}, bf16[24,2048]{1,0:T(8,128)(2,1)S(1)}, u32[]{:S(2)}, u32[]{:S(2)}) collective-permute-start(bf16[24,2048]{1,0:T(8,128)(2,1)S(1)} %get-tuple-element.122), channel_id=1, source_target_pairs={{0,3},{1,2},{2,1},{3,0},{4,7},{5,6},{6,5},{7,4},{8,11},{9,10},{10,... | collective-permute-start | bytes 294920 | tf_op jit(solution)/shard_map/ppermute | solution.py:38
  (20 other events, 117.1 us)
where the time goes:
time: 99.9 us; the launch traced here: 99.7 us
  starting transfers between devices  45.6 us (46%)
  waiting for transfers between devices  30.8 us (31%)
  Pallas kernels  21.2 us (21%)
  other arithmetic  1.72 us (2%)
    ppermute x30, starting transfers between devices, exchange(): lax.ppermute(pieces[step], axis, [(i, i ^ step) for i in range(size)])  44.6 us
    ppermute x30, waiting for transfers between devices, exchange(): lax.ppermute(pieces[step], axis, [(i, i ^ step) for i in range(size)])  30.8 us
    pallas_call x17, Pallas kernels, call(): pl.pallas_call(kernel, out_shape=[place(shape, dtype) for shape, dtype in...  21.2 us
  transfers between devices with their start and end apart: 33, of which 16 were waited for; matrix products, arithmetic and copies ran while one was open for 2% of the time, Pallas kernels for 19%

commit v1 on v0

--- a/solution.py
+++ b/solution.py
@@ -12,7 +12,6 @@
 rope_base = 1000000.0
 LANES = 128
 VMEM = pl.BlockSpec(memory_space=pltpu.VMEM)
-SMEM = pl.BlockSpec(memory_space=pltpu.SMEM)
 ANY = pl.BlockSpec(memory_space=pl.ANY)
 F32 = jnp.float32
 BF16 = jnp.bfloat16
@@ -39,7 +38,7 @@
     return got
 
 
-def fetch_kernel(count, _, *refs):
+def fetch_kernel(count, *refs):
     sources, targets, sems = refs[:count], refs[count : 2 * count], refs[2 * count]
     copies = [pltpu.make_async_copy(a, b, sems.at[i]) for i, (a, b) in enumerate(zip(sources, targets))]
     for copy in copies:
@@ -48,13 +47,13 @@
         copy.wait()
 
 
-def fetch(after, *arrays, held=True):
+def fetch(*arrays, held=True):
     moved = sum(a.size * a.dtype.itemsize for a in arrays)
     return call(
         functools.partial(fetch_kernel, len(arrays)),
         [(a.shape, a.dtype) for a in arrays],
-        [SMEM] + [ANY] * len(arrays),
-        [after] + [pltpu.with_memory_space_constraint(a, pltpu.HBM) if held else a for a in arrays],
+        [ANY] * len(arrays),
+        [pltpu.with_memory_space_constraint(a, pltpu.HBM) if held else a for a in arrays],
         scratch=[pltpu.SemaphoreType.DMA((len(arrays),))],
         cost=(0, moved),
         limit=1 << 20,
@@ -75,6 +74,16 @@
     rows = blocks[0].shape[0]
     query_width = w_query.shape[1]
     kv_width = w_keyvalue.shape[1]
+    picks = ids.shape[0]
+    spread = lax.broadcasted_iota(jnp.int32, (picks, LANES), 0) == lax.broadcasted_iota(jnp.int32, (picks, LANES), 1)
+    named = lax.dot_general(
+        ids[...].astype(F32).astype(BF16),
+        jnp.where(spread, 1.0, 0.0).astype(BF16),
+        (((0,), (0,)), ((), ())),
+        preferred_element_type=F32,
+    )
+    lane = lax.broadcasted_iota(jnp.int32, named.shape, 1)
+    named = jnp.where(lane < picks, named, -1.0).astype(BF16)
     normed = rms(stack(blocks), gain[...]).astype(BF16)
     queries = jnp.dot(normed, w_query[...], preferred_element_type=F32)
     fresh = jnp.dot(normed, w_keyvalue[...], preferred_element_type=F32)
@@ -82,7 +91,7 @@
         own = slice(step * rows, (step + 1) * rows)
         outs[step][:, :query_width] = queries[own].astype(BF16)
         outs[step][:, query_width : query_width + kv_width] = fresh[own].astype(BF16)
-        outs[step][:, query_width + kv_width :] = ids[...]
+        outs[step][:, query_width + kv_width :] = named
 
 
 def turn(values, gain, cosine, sine):
@@ -106,26 +115,27 @@
     return query.astype(F32), top, total, mixed
 
 
-def attend_kernel(steps, me_ref, *refs):
+def attend_kernel(steps, *refs):
     count = len(steps)
+    me = lax.axis_index("dev")
     messages = refs[:count]
     gain, cosine, sine, bias, keys, values = refs[count : count + 6]
     outs, scratch = refs[count + 7 : -1], refs[-1]
     for i, step in enumerate(steps):
         found = attend_cache(
-            messages[i], me_ref[0] ^ step, gain[...], cosine[...], sine[...], bias[...], keys, values, scratch.at[i]
+            messages[i], me ^ step, gain[...], cosine[...], sine[...], bias[...], keys, values, scratch.at[i]
         )
         for out, value in zip(outs[4 * i : 4 * i + 4], found):
             out[...] = jnp.broadcast_to(value, out.shape)
 
 
-def mix_kernel(count, done, me_ref, *refs):
+def mix_kernel(count, done, *refs):
     messages, parts = refs[:count], refs[count : count + 4 * done]
     refs = refs[count + 4 * done :]
     q_gain, k_gain, cosine, sine, bias, keys, values = refs[:7]
     outs = refs[7 : 7 + count]
     scratch, k_rot, v_new, kv_all = refs[7 + count :]
-    me = me_ref[0]
+    me = lax.axis_index("dev")
     rows, heads, _, dim = keys.shape
     group = scratch.shape[1] // rows
     query_width = group * dim
@@ -180,9 +190,9 @@
     ready[...] = rms(total, gain[...]).astype(BF16)
 
 
-def route_kernel(count, groups, capacity, where_ref, *refs):
+def route_kernel(count, groups, capacity, *refs):
     messages, outs = refs[:count], refs[count:]
-    dev, grp = where_ref[0], where_ref[1]
+    dev, grp = lax.axis_index("dev"), lax.axis_index("grp")
     rows, columns = messages[0].shape
     total = count * rows
     lane = lax.broadcasted_iota(jnp.int32, (total, LANES), 1)
@@ -288,7 +298,6 @@
     capacity = min(rows, max(3, (rows * picks + experts - 1) // experts + 1))
     strides = [max(8, count // 2 * capacity // 8 * 8)]
     strides.append(max(8, -(-(count * capacity - strides[0]) // 8) * 8))
-    where = jnp.stack([lax.axis_index("dev"), lax.axis_index("grp")])
 
     half = count // 2
     near, far = list(range(half)), list(range(half, count))
@@ -296,10 +305,24 @@
     own_weights = [w_gate[0], w_up[0], w_down[0]]
     gathered = exchange([tokens] * count, "dev", count)
     other_weights = [lax.ppermute(w, "role", swap) for w in own_weights]
-    query_kept, kv_kept, tokens_kept, gain_kept = fetch(where, w_query, w_keyvalue, tokens, norm_gain.reshape(1, -1))
+    query_kept, kv_kept, tokens_kept, gain_kept = fetch(w_query, w_keyvalue, tokens, norm_gain.reshape(1, -1))
     gathered[0] = tokens_kept
 
-    ids = jnp.pad(expert_ids.astype(BF16), ((0, 0), (0, LANES - picks)), constant_values=-1)
+    chunks = [near] + [[step] for step in far]
+    messages = [None] * count
+    for chunk in [near, far]:
+        made = call(
+            functools.partial(project_kernel, len(chunk)),
+            [((rows, query_width + kv_width + LANES), BF16)] * len(chunk),
+            [VMEM] * (len(chunk) + 4),
+            [*[gathered[step] for step in chunk], gain_kept, query_kept, kv_kept, expert_ids.T],
+            cost=(2 * len(chunk) * rows * width * (query_width + kv_width), 3 << 20),
+            limit=4 << 20,
+        )
+        if chunk == near:
+            lengths, made = lax.optimization_barrier((lengths, made))
+        for step, message in zip(chunk, made):
+            messages[step] = message
     frequency = rope_base ** (-jnp.arange(dim // 2, dtype=F32) / (dim // 2))
     angles = lengths.astype(F32)[:, None] * frequency[None, :]
     cosine, sine = jnp.cos(angles), jnp.sin(angles)
@@ -307,30 +330,16 @@
     sine = jnp.concatenate([-sine, sine], axis=1)
     visible = jnp.arange(places, dtype=jnp.int32)[None, :] < lengths[:, None]
     bias = jnp.where(visible, 0.0, -jnp.inf).astype(F32)
-
-    chunks = [near, far]
-    messages = [None] * count
-    for chunk in chunks:
-        made = call(
-            functools.partial(project_kernel, len(chunk)),
-            [((rows, query_width + kv_width + LANES), BF16)] * len(chunk),
-            [VMEM] * (len(chunk) + 4),
-            [*[gathered[step] for step in chunk], gain_kept, query_kept, kv_kept, ids],
-            cost=(2 * len(chunk) * rows * width * (query_width + kv_width), 3 << 20),
-            limit=4 << 20,
-        )
-        for step, message in zip(chunk, made):
-            messages[step] = message
     messages = exchange(messages, "dev", count)
     parts = []
     gains = [q_gain.reshape(1, -1), k_gain.reshape(1, -1)]
     flops = 4 * rows * group * places * dim
-    for chunk in chunks[:-1]:
+    for chunk in [near]:
         parts += call(
             functools.partial(attend_kernel, chunk),
             [((rows, group, dim), F32)] * (4 * len(chunk)),
-            [SMEM] + [VMEM] * (len(chunk) + 6) + [ANY],
-            [where, *[messages[step] for step in chunk], gains[0], cosine, sine, bias]
+            [VMEM] * (len(chunk) + 6) + [ANY],
+            [*[messages[step] for step in chunk], gains[0], cosine, sine, bias]
             + [cache_keys, cache_values, parts[-1] if parts else bias],
             scratch=[pltpu.VMEM((len(chunk), rows * group, dim), F32)],
             cost=(len(chunk) * flops, 2 << 20),
@@ -339,8 +348,8 @@
     mixtures = call(
         functools.partial(mix_kernel, count, half),
         [((rows, query_width), BF16)] * count,
-        [SMEM] + [VMEM] * (count + 4 * half + 7),
-        [where, *messages, *parts, *gains, cosine, sine, bias, cache_keys, cache_values],
+        [VMEM] * (count + 4 * half + 7),
+        [*messages, *parts, *gains, cosine, sine, bias, cache_keys, cache_values],
         scratch=[
             pltpu.VMEM((count, rows * group, dim), F32),
             pltpu.VMEM((heads, rows, dim), F32),
@@ -353,8 +362,8 @@
     choices = call(
         functools.partial(route_kernel, count, groups, capacity),
         [((half * rows, groups * strides[0]), BF16), ((count * rows, groups * strides[1]), BF16)],
-        [SMEM] + [VMEM] * count,
-        [where, *messages],
+        [VMEM] * count,
+        [*messages],
         cost=(0, 2 << 20),
         limit=2 << 20,
     )
@@ -381,7 +390,6 @@
         limit=8 << 20,
     )
     ready = exchange([ready] * count, "dev", count)
-    other_weights = fetch(where, *other_weights, held=False)
     results = []
     after = hidden
     for part, choice, stride in zip((near, near + far), choices, strides):

time: 99.9 us -> 102 us (1.021)
  starting transfers between devices: 45.6 us -> 56.2 us
  waiting for transfers between devices: 30.8 us -> 27 us
  Pallas kernels: 21.2 us -> 17.7 us
  other arithmetic: 1.72 us -> 0.29 us
    ppermute x30, starting transfers between devices: 44.6 us -> 55.2 us  [exchange(): lax.ppermute(pieces[step], axis, [(i, i ^ step) for i in range(size)])]
    ppermute x30, waiting for transfers between devices: 30.8 us -> 27 us  [exchange(): lax.ppermute(pieces[step], axis, [(i, i ^ step) for i in range(size)])]
    pallas_call x17, Pallas kernels: 21.2 us -> 17.7 us  [call(): pl.pallas_call(kernel, out_shape=[place(shape, dtype) for shape, dtype in...]
  transfers between devices with their start and end apart: 33 -> 33, of which waited for: 16 -> 16; matrix products, arithmetic and copies ran while one was open for 2% -> 0% of each run, Pallas kernels for 19% -> 15%
where the time goes in v1:
time: 102 us
  starting transfers between devices  56.2 us (55%)
  waiting for transfers between devices  27 us (26%)
  Pallas kernels  17.7 us (17%)
    ppermute x30, starting transfers between devices, exchange(): lax.ppermute(pieces[step], axis, [(i, i ^ step) for i in range(size)])  55.2 us
    ppermute x30, waiting for transfers between devices, exchange(): lax.ppermute(pieces[step], axis, [(i, i ^ step) for i in range(size)])  27 us
    pallas_call x17, Pallas kernels, call(): pl.pallas_call(kernel, out_shape=[place(shape, dtype) for shape, dtype in...  17.7 us
  transfers between devices with their start and end apart: 33, of which 16 were waited for; matrix products, arithmetic and copies ran while one was open for 0% of the time, Pallas kernels for 15%

profile of v1, /device:TPU:0, one launch (start us, length us, event | category | flops | bytes accessed | tf_op | source)
XLA Modules:
  0.0 101.5 jit_solution(9214084154919894592)
XLA Ops:
  1.0 2.6 %collective-permute-start = (bf16[24,2048]{1,0:T(8,128)(2,1)}, bf16[24,2048]{1,0:T(8,128)(2,1)S(1)}, u32[]{:S(2)}, u32[]{:S(2)}) collective-permute-start(bf16[24,2048]{1,0:T(8,128)(2,1)} %refs_2_.2), channel_id=1, source_target_pairs={{0,1},{1,0},{2,3},{3,2},{4,5},{5,4},{6,7},{7,6},{8,9},{9,8},{10,11... | collective-permute-start | bytes 294920 | tf_op jit(solution)/shard_map/ppermute | solution.py:37
  3.6 2.6 %collective-permute-start.2 = (bf16[24,2048]{1,0:T(8,128)(2,1)}, bf16[24,2048]{1,0:T(8,128)(2,1)S(1)}, u32[]{:S(2)}, u32[]{:S(2)}) collective-permute-start(bf16[24,2048]{1,0:T(8,128)(2,1)} %refs_2_.2), channel_id=1, source_target_pairs={{0,2},{1,3},{2,0},{3,1},{4,6},{5,7},{6,4},{7,5},{8,10},{9,11},{10,... | collective-permute-start | bytes 294920 | tf_op jit(solution)/shard_map/ppermute | solution.py:37
  6.2 2.6 %shard_map.145 = (bf16[2048,1024]{1,0:T(8,128)(2,1)S(1)}, bf16[2048,256]{1,0:T(8,128)(2,1)S(1)}, bf16[24,2048]{1,0:T(8,128)(2,1)S(1)}, f32[1,2048]{1,0:T(1,128)S(1)}) custom-call(bf16[2048,1024]{1,0:T(8,128)(2,1)} %refs_0_.1, bf16[2048,256]{1,0:T(8,128)(2,1)} %refs_1_.3, bf16[24,2048]{1,0:T(8,128)(2,1)} %refs_2_.2, f32[1,2048]{1,0:T(1,128)} %bitcast.23), custom_call_target="tpu_custom_call" | custom-call | bytes 5349376 | tf_op jit(solution)/shard_map/pallas_call | solution.py:23
  8.7 3.3 %collective-permute-start.3 = (bf16[24,2048]{1,0:T(8,128)(2,1)S(1)}, bf16[24,2048]{1,0:T(8,128)(2,1)S(1)}, u32[]{:S(2)}, u32[]{:S(2)}) collective-permute-start(bf16[24,2048]{1,0:T(8,128)(2,1)S(1)} %copy-done.10), channel_id=1, source_target_pairs={{0,3},{1,2},{2,1},{3,0},{4,7},{5,6},{6,5},{7,4},{8,11},{9,10},{10,... | collective-permute-start | bytes 294920 | tf_op jit(solution)/shard_map/ppermute | solution.py:37
  13.4 2.7 %collective-permute-done.3.refs_1_ = bf16[24,2048]{1,0:T(8,128)(2,1)S(1)} collective-permute-done((bf16[24,2048]{1,0:T(8,128)(2,1)S(1)}, bf16[24,2048]{1,0:T(8,128)(2,1)S(1)}, u32[]{:S(2)}, u32[]{:S(2)}) %collective-permute-start.3) | collective-permute-done | bytes 98336 | tf_op jit(solution)/shard_map/ppermute | solution.py:37
  17.9 2.7 %collective-permute-start.5 = (bf16[24,1408]{1,0:T(8,128)(2,1)S(1)}, bf16[24,1408]{1,0:T(8,128)(2,1)S(1)}, u32[]{:S(2)}, u32[]{:S(2)}) collective-permute-start(bf16[24,1408]{1,0:T(8,128)(2,1)S(1)} %get-tuple-element.71), channel_id=1, source_target_pairs={{0,3},{1,2},{2,1},{3,0},{4,7},{5,6},{6,5},{7,4},{8,11},{9,10},{10,... | collective-permute-start | bytes 202760 | tf_op jit(solution)/shard_map/ppermute | solution.py:37
  22.2 2.1 %collective-permute-done.4.refs_2_ = bf16[24,1408]{1,0:T(8,128)(2,1)S(1)} collective-permute-done((bf16[24,1408]{1,0:T(8,128)(2,1)S(1)}, bf16[24,1408]{1,0:T(8,128)(2,1)S(1)}, u32[]{:S(2)}, u32[]{:S(2)}) %collective-permute-start.4) | collective-permute-done | bytes 67616 | tf_op jit(solution)/shard_map/ppermute | solution.py:37
  24.3 2.7 %shard_map.149 = (bf16[24,1024]{1,0:T(8,128)(2,1)S(1)}, bf16[24,1024]{1,0:T(8,128)(2,1)S(1)}, bf16[24,1024]{1,0:T(8,128)(2,1)S(1)}, bf16[24,1024]{1,0:T(8,128)(2,1)S(1)}) custom-call(bf16[24,1408]{1,0:T(8,128)(2,1)S(1)} %get-tuple-element.68.refs_0_, bf16[24,1408]{1,0:T(8,128)(2,1)S(1)} %collective-permute-done.1.refs_1_, ...), custom_call_target="tpu_custom_call" | custom-call | flops 12582912 | bytes 2097152 | tf_op jit(solution)/shard_map/pallas_call | solution.py:23
  33.9 3.0 %collective-permute-start.10 = (bf16[24,1024]{1,0:T(8,128)(2,1)S(1)}, bf16[24,1024]{1,0:T(8,128)(2,1)S(1)}, u32[]{:S(2)}, u32[]{:S(2)}) collective-permute-start(bf16[24,1024]{1,0:T(8,128)(2,1)S(1)} %get-tuple-element.86), channel_id=1, source_target_pairs={{0,3},{1,2},{2,1},{3,0},{4,7},{5,6},{6,5},{7,4},{8,11},{9,10},{10,... | collective-permute-start | bytes 147464 | tf_op jit(solution)/shard_map/ppermute | solution.py:37
  37.7 2.1 %collective-permute-done.10.refs_0_ = bf16[24,1024]{1,0:T(8,128)(2,1)S(1)} collective-permute-done((bf16[24,1024]{1,0:T(8,128)(2,1)S(1)}, bf16[24,1024]{1,0:T(8,128)(2,1)S(1)}, u32[]{:S(2)}, u32[]{:S(2)}) %collective-permute-start.10) | collective-permute-done | bytes 49184 | tf_op jit(solution)/shard_map/ppermute | solution.py:37
  39.8 3.2 %collective-permute-start.9 = (bf16[24,2048]{1,0:T(8,128)(2,1)S(1)}, bf16[24,2048]{1,0:T(8,128)(2,1)S(1)}, u32[]{:S(2)}, u32[]{:S(2)}) collective-permute-start(bf16[24,2048]{1,0:T(8,128)(2,1)S(1)} %shard_map.151), channel_id=1, source_target_pairs={{0,2},{1,3},{2,0},{3,1},{4,6},{5,7},{6,4},{7,5},{8,10},{9,11},{10,... | collective-permute-start | bytes 294920 | tf_op jit(solution)/shard_map/ppermute | solution.py:37
  44.3 2.3 %collective-permute-done.9.refs_2_ = bf16[24,2048]{1,0:T(8,128)(2,1)S(1)} collective-permute-done((bf16[24,2048]{1,0:T(8,128)(2,1)S(1)}, bf16[24,2048]{1,0:T(8,128)(2,1)S(1)}, u32[]{:S(2)}, u32[]{:S(2)}) %collective-permute-start.9) | collective-permute-done | bytes 98336 | tf_op jit(solution)/shard_map/ppermute | solution.py:37
  46.6 3.7 %collective-permute-done.11.refs_3_ = bf16[24,2048]{1,0:T(8,128)(2,1)S(1)} collective-permute-done((bf16[24,2048]{1,0:T(8,128)(2,1)S(1)}, bf16[24,2048]{1,0:T(8,128)(2,1)S(1)}, u32[]{:S(2)}, u32[]{:S(2)}) %collective-permute-start.11) | collective-permute-done | bytes 98336 | tf_op jit(solution)/shard_map/ppermute | solution.py:37
  50.4 2.8 %collective-permute-start.12 = (bf16[24,2048]{1,0:T(8,128)(2,1)S(1)}, bf16[24,2048]{1,0:T(8,128)(2,1)S(1)}, u32[]{:S(2)}, u32[]{:S(2)}) collective-permute-start(bf16[24,2048]{1,0:T(8,128)(2,1)S(1)} %get-tuple-element.87.refs_0_), channel_id=1, source_target_pairs={{0,1},{1,0},{2,3},{3,2},{4,5},{5,4},{6,7},{7,6},{8,9},{9,8},{10,11... | collective-permute-start | bytes 294920 | tf_op jit(solution)/shard_map/ppermute | solution.py:37
  55.8 3.0 %collective-permute-start.20 = (bf16[24,2048]{1,0:T(8,128)(2,1)S(1)}, bf16[24,2048]{1,0:T(8,128)(2,1)S(1)}, u32[]{:S(2)}, u32[]{:S(2)}) collective-permute-start(bf16[24,2048]{1,0:T(8,128)(2,1)S(1)} %get-tuple-element.87.refs_0_), channel_id=1, source_target_pairs={{0,3},{1,2},{2,1},{3,0},{4,7},{5,6},{6,5},{7,4},{8,11},{9,10},{10,... | collective-permute-start | bytes 294920 | tf_op jit(solution)/shard_map/ppermute | solution.py:37
  63.9 2.5 %collective-permute-start.15 = (bf16[24,2048]{1,0:T(8,128)(2,1)S(1)}, bf16[24,2048]{1,0:T(8,128)(2,1)S(1)}, u32[]{:S(2)}, u32[]{:S(2)}) collective-permute-start(bf16[24,2048]{1,0:T(8,128)(2,1)S(1)} %get-tuple-element.93), channel_id=1, source_target_pairs={{0,12},{4,8},{8,4},{12,0},{1,13},{5,9},{9,5},{13,1},{2,14},{6,10},... | collective-permute-start | bytes 294920 | tf_op jit(solution)/shard_map/ppermute | solution.py:37
  68.6 1.9 %collective-permute-done.15.refs_3_ = bf16[24,2048]{1,0:T(8,128)(2,1)S(1)} collective-permute-done((bf16[24,2048]{1,0:T(8,128)(2,1)S(1)}, bf16[24,2048]{1,0:T(8,128)(2,1)S(1)}, u32[]{:S(2)}, u32[]{:S(2)}) %collective-permute-start.15) | collective-permute-done | bytes 98336 | tf_op jit(solution)/shard_map/ppermute | solution.py:37
  71.4 2.3 %collective-permute-start.23 = (bf16[32,2048]{1,0:T(8,128)(2,1)S(1)}, bf16[32,2048]{1,0:T(8,128)(2,1)S(1)}, u32[]{:S(2)}, u32[]{:S(2)}) collective-permute-start(bf16[32,2048]{1,0:T(8,128)(2,1)S(1)} %get-tuple-element.102), channel_id=1, source_target_pairs={{0,12},{4,8},{8,4},{12,0},{1,13},{5,9},{9,5},{13,1},{2,14},{6,10},... | collective-permute-start | bytes 393224 | tf_op jit(solution)/shard_map/ppermute | solution.py:37
  75.5 2.3 %collective-permute-done.22.refs_2_ = bf16[32,2048]{1,0:T(8,128)(2,1)S(1)} collective-permute-done((bf16[32,2048]{1,0:T(8,128)(2,1)S(1)}, bf16[32,2048]{1,0:T(8,128)(2,1)S(1)}, u32[]{:S(2)}, u32[]{:S(2)}) %collective-permute-start.22) | collective-permute-done | bytes 131104 | tf_op jit(solution)/shard_map/ppermute | solution.py:37
  77.9 1.9 %shard_map.158 = (bf16[32,2048]{1,0:T(8,128)(2,1)S(1)}, bf16[32,2048]{1,0:T(8,128)(2,1)S(1)}, bf16[32,2048]{1,0:T(8,128)(2,1)S(1)}, bf16[32,2048]{1,0:T(8,128)(2,1)S(1)}) custom-call(bf16[32,2048]{1,0:T(8,128)(2,1)S(1)} %get-tuple-element.99.refs_0_, bf16[32,2048]{1,0:T(8,128)(2,1)S(1)} %collective-permute-done.21.refs_1_, ...), custom_call_target="tpu_custom_call" | custom-call | flops 1207959552 | bytes 4194304 | tf_op jit(solution)/shard_map/pallas_call | solution.py:23
  88.5 2.4 %collective-permute-start.31 = (bf16[24,2048]{1,0:T(8,128)(2,1)S(1)}, bf16[24,2048]{1,0:T(8,128)(2,1)S(1)}, u32[]{:S(2)}, u32[]{:S(2)}) collective-permute-start(bf16[24,2048]{1,0:T(8,128)(2,1)S(1)} %get-tuple-element.115.refs_10_), channel_id=1, source_target_pairs={{0,2},{1,3},{2,0},{3,1},{4,6},{5,7},{6,4},{7,5},{8,10},{9,11},{10,... | collective-permute-start | bytes 294920 | tf_op jit(solution)/shard_map/ppermute | solution.py:37
  91.7 2.8 %collective-permute-start.30 = (bf16[24,2048]{1,0:T(8,128)(2,1)S(1)}, bf16[24,2048]{1,0:T(8,128)(2,1)S(1)}, u32[]{:S(2)}, u32[]{:S(2)}) collective-permute-start(bf16[24,2048]{1,0:T(8,128)(2,1)S(1)} %get-tuple-element.117), channel_id=1, source_target_pairs={{0,1},{1,0},{2,3},{3,2},{4,5},{5,4},{6,7},{7,6},{8,9},{9,8},{10,11... | collective-permute-start | bytes 294920 | tf_op jit(solution)/shard_map/ppermute | solution.py:37
  94.4 2.1 %collective-permute-start.32 = (bf16[24,2048]{1,0:T(8,128)(2,1)S(1)}, bf16[24,2048]{1,0:T(8,128)(2,1)S(1)}, u32[]{:S(2)}, u32[]{:S(2)}) collective-permute-start(bf16[24,2048]{1,0:T(8,128)(2,1)S(1)} %get-tuple-element.118), channel_id=1, source_target_pairs={{0,3},{1,2},{2,1},{3,0},{4,7},{5,6},{6,5},{7,4},{8,11},{9,10},{10,... | collective-permute-start | bytes 294920 | tf_op jit(solution)/shard_map/ppermute | solution.py:37
  97.0 3.8 %collective-permute-done.32.refs_3_ = bf16[24,2048]{1,0:T(8,128)(2,1)S(1)} collective-permute-done((bf16[24,2048]{1,0:T(8,128)(2,1)S(1)}, bf16[24,2048]{1,0:T(8,128)(2,1)S(1)}, u32[]{:S(2)}, u32[]{:S(2)}) %collective-permute-start.32) | collective-permute-done | bytes 98336 | tf_op jit(solution)/shard_map/ppermute | solution.py:37
  (88 shorter events, 38.0 us)
Async XLA Ops:
  0.0 71.4 %collective-permute-start.16 = (bf16[2048,384]{1,0:T(8,128)(2,1)}, bf16[2048,384]{1,0:T(8,128)(2,1)S(1)}, u32[]{:S(2)}, u32[]{:S(2)}) collective-permute-start(bf16[2048,384]{1,0:T(8,128)(2,1)} %bitcast.8), channel_id=1, source_target_pairs={{0,16},{16,0},{1,17},{17,1},{2,18},{18,2},{3,19},{19,3},{4,20},{20... | collective-permute-start | bytes 4718600 | tf_op jit(solution)/shard_map/ppermute | solution.py:307
  0.5 73.2 %collective-permute-start.17 = (bf16[2048,384]{1,0:T(8,128)(2,1)}, bf16[2048,384]{1,0:T(8,128)(2,1)S(1)}, u32[]{:S(2)}, u32[]{:S(2)}) collective-permute-start(bf16[2048,384]{1,0:T(8,128)(2,1)} %bitcast.11), channel_id=1, source_target_pairs={{0,16},{16,0},{1,17},{17,1},{2,18},{18,2},{3,19},{19,3},{4,20},{20... | collective-permute-start | bytes 4718600 | tf_op jit(solution)/shard_map/ppermute | solution.py:307
  0.5 73.1 %collective-permute-start.18 = (bf16[384,2048]{1,0:T(8,128)(2,1)}, bf16[384,2048]{1,0:T(8,128)(2,1)S(1)}, u32[]{:S(2)}, u32[]{:S(2)}) collective-permute-start(bf16[384,2048]{1,0:T(8,128)(2,1)} %bitcast.14), channel_id=1, source_target_pairs={{0,16},{16,0},{1,17},{17,1},{2,18},{18,2},{3,19},{19,3},{4,20},{20... | collective-permute-start | bytes 4718600 | tf_op jit(solution)/shard_map/ppermute | solution.py:307
  1.0 7.7 %collective-permute-start = (bf16[24,2048]{1,0:T(8,128)(2,1)}, bf16[24,2048]{1,0:T(8,128)(2,1)S(1)}, u32[]{:S(2)}, u32[]{:S(2)}) collective-permute-start(bf16[24,2048]{1,0:T(8,128)(2,1)} %refs_2_.2), channel_id=1, source_target_pairs={{0,1},{1,0},{2,3},{3,2},{4,5},{5,4},{6,7},{7,6},{8,9},{9,8},{10,11... | collective-permute-start | bytes 294920 | tf_op jit(solution)/shard_map/ppermute | solution.py:37
  3.6 9.7 %collective-permute-start.2 = (bf16[24,2048]{1,0:T(8,128)(2,1)}, bf16[24,2048]{1,0:T(8,128)(2,1)S(1)}, u32[]{:S(2)}, u32[]{:S(2)}) collective-permute-start(bf16[24,2048]{1,0:T(8,128)(2,1)} %refs_2_.2), channel_id=1, source_target_pairs={{0,2},{1,3},{2,0},{3,1},{4,6},{5,7},{6,4},{7,5},{8,10},{9,11},{10,... | collective-permute-start | bytes 294920 | tf_op jit(solution)/shard_map/ppermute | solution.py:37
  8.7 7.3 %collective-permute-start.3 = (bf16[24,2048]{1,0:T(8,128)(2,1)S(1)}, bf16[24,2048]{1,0:T(8,128)(2,1)S(1)}, u32[]{:S(2)}, u32[]{:S(2)}) collective-permute-start(bf16[24,2048]{1,0:T(8,128)(2,1)S(1)} %copy-done.10), channel_id=1, source_target_pairs={{0,3},{1,2},{2,1},{3,0},{4,7},{5,6},{6,5},{7,4},{8,11},{9,10},{10,... | collective-permute-start | bytes 294920 | tf_op jit(solution)/shard_map/ppermute | solution.py:37
  17.2 7.1 %collective-permute-start.4 = (bf16[24,1408]{1,0:T(8,128)(2,1)S(1)}, bf16[24,1408]{1,0:T(8,128)(2,1)S(1)}, u32[]{:S(2)}, u32[]{:S(2)}) collective-permute-start(bf16[24,1408]{1,0:T(8,128)(2,1)S(1)} %get-tuple-element.70), channel_id=1, source_target_pairs={{0,2},{1,3},{2,0},{3,1},{4,6},{5,7},{6,4},{7,5},{8,10},{9,11},{10,... | collective-permute-start | bytes 202760 | tf_op jit(solution)/shard_map/ppermute | solution.py:37
  17.9 6.4 %collective-permute-start.5 = (bf16[24,1408]{1,0:T(8,128)(2,1)S(1)}, bf16[24,1408]{1,0:T(8,128)(2,1)S(1)}, u32[]{:S(2)}, u32[]{:S(2)}) collective-permute-start(bf16[24,1408]{1,0:T(8,128)(2,1)S(1)} %get-tuple-element.71), channel_id=1, source_target_pairs={{0,3},{1,2},{2,1},{3,0},{4,7},{5,6},{6,5},{7,4},{8,11},{9,10},{10,... | collective-permute-start | bytes 202760 | tf_op jit(solution)/shard_map/ppermute | solution.py:37
  32.1 11.7 %collective-permute-start.7 = (bf16[24,2048]{1,0:T(8,128)(2,1)S(1)}, bf16[24,2048]{1,0:T(8,128)(2,1)S(1)}, u32[]{:S(2)}, u32[]{:S(2)}) collective-permute-start(bf16[24,2048]{1,0:T(8,128)(2,1)S(1)} %get-tuple-element.84), channel_id=1, source_target_pairs={{0,1},{1,0},{2,3},{3,2},{4,5},{5,4},{6,7},{7,6},{8,9},{9,8},{10,11... | collective-permute-start | bytes 294920 | tf_op jit(solution)/shard_map/ppermute | solution.py:37
  33.9 5.9 %collective-permute-start.10 = (bf16[24,1024]{1,0:T(8,128)(2,1)S(1)}, bf16[24,1024]{1,0:T(8,128)(2,1)S(1)}, u32[]{:S(2)}, u32[]{:S(2)}) collective-permute-start(bf16[24,1024]{1,0:T(8,128)(2,1)S(1)} %get-tuple-element.86), channel_id=1, source_target_pairs={{0,3},{1,2},{2,1},{3,0},{4,7},{5,6},{6,5},{7,4},{8,11},{9,10},{10,... | collective-permute-start | bytes 147464 | tf_op jit(solution)/shard_map/ppermute | solution.py:37
  39.8 6.8 %collective-permute-start.9 = (bf16[24,2048]{1,0:T(8,128)(2,1)S(1)}, bf16[24,2048]{1,0:T(8,128)(2,1)S(1)}, u32[]{:S(2)}, u32[]{:S(2)}) collective-permute-start(bf16[24,2048]{1,0:T(8,128)(2,1)S(1)} %shard_map.151), channel_id=1, source_target_pairs={{0,2},{1,3},{2,0},{3,1},{4,6},{5,7},{6,4},{7,5},{8,10},{9,11},{10,... | collective-permute-start | bytes 294920 | tf_op jit(solution)/shard_map/ppermute | solution.py:37
  43.8 6.5 %collective-permute-start.11 = (bf16[24,2048]{1,0:T(8,128)(2,1)S(1)}, bf16[24,2048]{1,0:T(8,128)(2,1)S(1)}, u32[]{:S(2)}, u32[]{:S(2)}) collective-permute-start(bf16[24,2048]{1,0:T(8,128)(2,1)S(1)} %shard_map.152), channel_id=1, source_target_pairs={{0,3},{1,2},{2,1},{3,0},{4,7},{5,6},{6,5},{7,4},{8,11},{9,10},{10,... | collective-permute-start | bytes 294920 | tf_op jit(solution)/shard_map/ppermute | solution.py:37
  53.2 5.9 %collective-permute-start.19 = (bf16[24,2048]{1,0:T(8,128)(2,1)S(1)}, bf16[24,2048]{1,0:T(8,128)(2,1)S(1)}, u32[]{:S(2)}, u32[]{:S(2)}) collective-permute-start(bf16[24,2048]{1,0:T(8,128)(2,1)S(1)} %get-tuple-element.87.refs_0_), channel_id=1, source_target_pairs={{0,2},{1,3},{2,0},{3,1},{4,6},{5,7},{6,4},{7,5},{8,10},{9,11},{10,... | collective-permute-start | bytes 294920 | tf_op jit(solution)/shard_map/ppermute | solution.py:37
  55.8 6.5 %collective-permute-start.20 = (bf16[24,2048]{1,0:T(8,128)(2,1)S(1)}, bf16[24,2048]{1,0:T(8,128)(2,1)S(1)}, u32[]{:S(2)}, u32[]{:S(2)}) collective-permute-start(bf16[24,2048]{1,0:T(8,128)(2,1)S(1)} %get-tuple-element.87.refs_0_), channel_id=1, source_target_pairs={{0,3},{1,2},{2,1},{3,0},{4,7},{5,6},{6,5},{7,4},{8,11},{9,10},{10,... | collective-permute-start | bytes 294920 | tf_op jit(solution)/shard_map/ppermute | solution.py:37
  63.9 6.6 %collective-permute-start.15 = (bf16[24,2048]{1,0:T(8,128)(2,1)S(1)}, bf16[24,2048]{1,0:T(8,128)(2,1)S(1)}, u32[]{:S(2)}, u32[]{:S(2)}) collective-permute-start(bf16[24,2048]{1,0:T(8,128)(2,1)S(1)} %get-tuple-element.93), channel_id=1, source_target_pairs={{0,12},{4,8},{8,4},{12,0},{1,13},{5,9},{9,5},{13,1},{2,14},{6,10},... | collective-permute-start | bytes 294920 | tf_op jit(solution)/shard_map/ppermute | solution.py:37
  67.0 8.6 %collective-permute-start.21 = (bf16[32,2048]{1,0:T(8,128)(2,1)S(1)}, bf16[32,2048]{1,0:T(8,128)(2,1)S(1)}, u32[]{:S(2)}, u32[]{:S(2)}) collective-permute-start(bf16[32,2048]{1,0:T(8,128)(2,1)S(1)} %get-tuple-element.100), channel_id=1, source_target_pairs={{0,4},{4,0},{8,12},{12,8},{1,5},{5,1},{9,13},{13,9},{2,6},{6,2},{1... | collective-permute-start | bytes 393224 | tf_op jit(solution)/shard_map/ppermute | solution.py:37
  70.5 7.4 %collective-permute-start.22 = (bf16[32,2048]{1,0:T(8,128)(2,1)S(1)}, bf16[32,2048]{1,0:T(8,128)(2,1)S(1)}, u32[]{:S(2)}, u32[]{:S(2)}) collective-permute-start(bf16[32,2048]{1,0:T(8,128)(2,1)S(1)} %get-tuple-element.101), channel_id=1, source_target_pairs={{0,8},{4,12},{8,0},{12,4},{1,9},{5,13},{9,1},{13,5},{2,10},{6,14},... | collective-permute-start | bytes 393224 | tf_op jit(solution)/shard_map/ppermute | solution.py:37
  71.4 6.5 %collective-permute-start.23 = (bf16[32,2048]{1,0:T(8,128)(2,1)S(1)}, bf16[32,2048]{1,0:T(8,128)(2,1)S(1)}, u32[]{:S(2)}, u32[]{:S(2)}) collective-permute-start(bf16[32,2048]{1,0:T(8,128)(2,1)S(1)} %get-tuple-element.102), channel_id=1, source_target_pairs={{0,12},{4,8},{8,4},{12,0},{1,13},{5,9},{9,5},{13,1},{2,14},{6,10},... | collective-permute-start | bytes 393224 | tf_op jit(solution)/shard_map/ppermute | solution.py:37
  79.8 6.0 %collective-permute-start.27 = (bf16[32,2048]{1,0:T(8,128)(2,1)S(1)}, bf16[32,2048]{1,0:T(8,128)(2,1)S(1)}, u32[]{:S(2)}, u32[]{:S(2)}) collective-permute-start(bf16[32,2048]{1,0:T(8,128)(2,1)S(1)} %get-tuple-element.112), channel_id=1, source_target_pairs={{0,4},{4,0},{8,12},{12,8},{1,5},{5,1},{9,13},{13,9},{2,6},{6,2},{1... | collective-permute-start | bytes 393224 | tf_op jit(solution)/shard_map/ppermute | solution.py:37
  82.4 5.9 %collective-permute-start.29 = (bf16[32,2048]{1,0:T(8,128)(2,1)S(1)}, bf16[32,2048]{1,0:T(8,128)(2,1)S(1)}, u32[]{:S(2)}, u32[]{:S(2)}) collective-permute-start(bf16[32,2048]{1,0:T(8,128)(2,1)S(1)} %get-tuple-element.114), channel_id=1, source_target_pairs={{0,12},{4,8},{8,4},{12,0},{1,13},{5,9},{9,5},{13,1},{2,14},{6,10},... | collective-permute-start | bytes 393224 | tf_op jit(solution)/shard_map/ppermute | solution.py:37
  83.4 7.5 %collective-permute-start.24 = (bf16[24,2048]{1,0:T(8,128)(2,1)S(1)}, bf16[24,2048]{1,0:T(8,128)(2,1)S(1)}, u32[]{:S(2)}, u32[]{:S(2)}) collective-permute-start(bf16[24,2048]{1,0:T(8,128)(2,1)S(1)} %get-tuple-element.108), channel_id=1, source_target_pairs={{0,4},{4,0},{8,12},{12,8},{1,5},{5,1},{9,13},{13,9},{2,6},{6,2},{1... | collective-permute-start | bytes 294920 | tf_op jit(solution)/shard_map/ppermute | solution.py:37
  85.1 5.8 %collective-permute-start.25 = (bf16[24,2048]{1,0:T(8,128)(2,1)S(1)}, bf16[24,2048]{1,0:T(8,128)(2,1)S(1)}, u32[]{:S(2)}, u32[]{:S(2)}) collective-permute-start(bf16[24,2048]{1,0:T(8,128)(2,1)S(1)} %get-tuple-element.109), channel_id=1, source_target_pairs={{0,8},{4,12},{8,0},{12,4},{1,9},{5,13},{9,1},{13,5},{2,10},{6,14},... | collective-permute-start | bytes 294920 | tf_op jit(solution)/shard_map/ppermute | solution.py:37
  88.5 8.6 %collective-permute-start.31 = (bf16[24,2048]{1,0:T(8,128)(2,1)S(1)}, bf16[24,2048]{1,0:T(8,128)(2,1)S(1)}, u32[]{:S(2)}, u32[]{:S(2)}) collective-permute-start(bf16[24,2048]{1,0:T(8,128)(2,1)S(1)} %get-tuple-element.115.refs_10_), channel_id=1, source_target_pairs={{0,2},{1,3},{2,0},{3,1},{4,6},{5,7},{6,4},{7,5},{8,10},{9,11},{10,... | collective-permute-start | bytes 294920 | tf_op jit(solution)/shard_map/ppermute | solution.py:37
  94.4 6.4 %collective-permute-start.32 = (bf16[24,2048]{1,0:T(8,128)(2,1)S(1)}, bf16[24,2048]{1,0:T(8,128)(2,1)S(1)}, u32[]{:S(2)}, u32[]{:S(2)}) collective-permute-start(bf16[24,2048]{1,0:T(8,128)(2,1)S(1)} %get-tuple-element.118), channel_id=1, source_target_pairs={{0,3},{1,2},{2,1},{3,0},{4,7},{5,6},{6,5},{7,4},{8,11},{9,10},{10,... | collective-permute-start | bytes 294920 | tf_op jit(solution)/shard_map/ppermute | solution.py:37
  (21 other events, 196.2 us)

commit v2 on v1

--- a/solution.py
+++ b/solution.py
@@ -334,7 +334,7 @@
     parts = []
     gains = [q_gain.reshape(1, -1), k_gain.reshape(1, -1)]
     flops = 4 * rows * group * places * dim
-    for chunk in [near]:
+    for chunk in chunks[:-1]:
         parts += call(
             functools.partial(attend_kernel, chunk),
             [((rows, group, dim), F32)] * (4 * len(chunk)),
@@ -346,9 +346,9 @@
             limit=4 << 20,
         )
     mixtures = call(
-        functools.partial(mix_kernel, count, half),
+        functools.partial(mix_kernel, count, count - 1),
         [((rows, query_width), BF16)] * count,
-        [VMEM] * (count + 4 * half + 7),
+        [VMEM] * (count + 4 * (count - 1) + 7),
         [*messages, *parts, *gains, cosine, sine, bias, cache_keys, cache_values],
         scratch=[
             pltpu.VMEM((count, rows * group, dim), F32),
@@ -413,7 +413,6 @@
                 limit=8 << 20,
             )
         )
-    results = lax.optimization_barrier(results)
     sums = [None] * count
     after = hidden
     held = [None, exchange(results[1], "grp", groups)]

time: 102 us -> 101 us (level)
  starting transfers between devices: 56.2 us -> 50.6 us
  waiting for transfers between devices: 27 us -> 31.7 us
    ppermute x30, starting transfers between devices: 55.2 us -> 49.6 us  [exchange(): lax.ppermute(pieces[step], axis, [(i, i ^ step) for i in range(size)])]
    ppermute x30, waiting for transfers between devices: 27 us -> 31.7 us  [exchange(): lax.ppermute(pieces[step], axis, [(i, i ^ step) for i in range(size)])]
    pallas_call x17 -> x18, Pallas kernels: 17.7 us -> 17.9 us  [call(): pl.pallas_call(kernel, out_shape=[place(shape, dtype) for shape, dtype in...]
  transfers between devices with their start and end apart: 33 -> 33, of which waited for: 16 -> 15; matrix products, arithmetic and copies ran while one was open for 0% -> 0% of each run, Pallas kernels for 15% -> 17%
where the time goes in v2:
time: 101 us
  starting transfers between devices  50.6 us (50%)
  waiting for transfers between devices  31.7 us (31%)
  Pallas kernels  17.9 us (18%)
    ppermute x30, starting transfers between devices, exchange(): lax.ppermute(pieces[step], axis, [(i, i ^ step) for i in range(size)])  49.6 us
    ppermute x30, waiting for transfers between devices, exchange(): lax.ppermute(pieces[step], axis, [(i, i ^ step) for i in range(size)])  31.7 us
    pallas_call x18, Pallas kernels, call(): pl.pallas_call(kernel, out_shape=[place(shape, dtype) for shape, dtype in...  17.9 us
  transfers between devices with their start and end apart: 33, of which 15 were waited for; matrix products, arithmetic and copies ran while one was open for 0% of the time, Pallas kernels for 17%

profile of v2, /device:TPU:0, one launch (start us, length us, event | category | flops | bytes accessed | tf_op | source)
XLA Modules:
  0.0 100.9 jit_solution(785439940452784910)
XLA Ops:
  1.0 2.6 %collective-permute-start = (bf16[24,2048]{1,0:T(8,128)(2,1)}, bf16[24,2048]{1,0:T(8,128)(2,1)S(1)}, u32[]{:S(2)}, u32[]{:S(2)}) collective-permute-start(bf16[24,2048]{1,0:T(8,128)(2,1)} %refs_2_.2), channel_id=1, source_target_pairs={{0,1},{1,0},{2,3},{3,2},{4,5},{5,4},{6,7},{7,6},{8,9},{9,8},{10,11... | collective-permute-start | bytes 294920 | tf_op jit(solution)/shard_map/ppermute | solution.py:37
  3.6 2.6 %collective-permute-start.2 = (bf16[24,2048]{1,0:T(8,128)(2,1)}, bf16[24,2048]{1,0:T(8,128)(2,1)S(1)}, u32[]{:S(2)}, u32[]{:S(2)}) collective-permute-start(bf16[24,2048]{1,0:T(8,128)(2,1)} %refs_2_.2), channel_id=1, source_target_pairs={{0,2},{1,3},{2,0},{3,1},{4,6},{5,7},{6,4},{7,5},{8,10},{9,11},{10,... | collective-permute-start | bytes 294920 | tf_op jit(solution)/shard_map/ppermute | solution.py:37
  6.2 2.6 %shard_map.145 = (bf16[2048,1024]{1,0:T(8,128)(2,1)S(1)}, bf16[2048,256]{1,0:T(8,128)(2,1)S(1)}, bf16[24,2048]{1,0:T(8,128)(2,1)S(1)}, f32[1,2048]{1,0:T(1,128)S(1)}) custom-call(bf16[2048,1024]{1,0:T(8,128)(2,1)} %refs_0_.1, bf16[2048,256]{1,0:T(8,128)(2,1)} %refs_1_.3, bf16[24,2048]{1,0:T(8,128)(2,1)} %refs_2_.2, f32[1,2048]{1,0:T(1,128)} %bitcast.24), custom_call_target="tpu_custom_call" | custom-call | bytes 5349376 | tf_op jit(solution)/shard_map/pallas_call | solution.py:23
  8.7 3.3 %collective-permute-start.3 = (bf16[24,2048]{1,0:T(8,128)(2,1)S(1)}, bf16[24,2048]{1,0:T(8,128)(2,1)S(1)}, u32[]{:S(2)}, u32[]{:S(2)}) collective-permute-start(bf16[24,2048]{1,0:T(8,128)(2,1)S(1)} %copy-done.10), channel_id=1, source_target_pairs={{0,3},{1,2},{2,1},{3,0},{4,7},{5,6},{6,5},{7,4},{8,11},{9,10},{10,... | collective-permute-start | bytes 294920 | tf_op jit(solution)/shard_map/ppermute | solution.py:37
  13.3 2.8 %collective-permute-done.3.refs_1_ = bf16[24,2048]{1,0:T(8,128)(2,1)S(1)} collective-permute-done((bf16[24,2048]{1,0:T(8,128)(2,1)S(1)}, bf16[24,2048]{1,0:T(8,128)(2,1)S(1)}, u32[]{:S(2)}, u32[]{:S(2)}) %collective-permute-start.3) | collective-permute-done | bytes 98336 | tf_op jit(solution)/shard_map/ppermute | solution.py:37
  17.9 2.7 %collective-permute-start.5 = (bf16[24,1408]{1,0:T(8,128)(2,1)S(1)}, bf16[24,1408]{1,0:T(8,128)(2,1)S(1)}, u32[]{:S(2)}, u32[]{:S(2)}) collective-permute-start(bf16[24,1408]{1,0:T(8,128)(2,1)S(1)} %get-tuple-element.67), channel_id=1, source_target_pairs={{0,3},{1,2},{2,1},{3,0},{4,7},{5,6},{6,5},{7,4},{8,11},{9,10},{10,... | collective-permute-start | bytes 202760 | tf_op jit(solution)/shard_map/ppermute | solution.py:37
  22.2 2.1 %collective-permute-done.4.refs_0_.refs_2_ = bf16[24,1408]{1,0:T(8,128)(2,1)S(1)} collective-permute-done((bf16[24,1408]{1,0:T(8,128)(2,1)S(1)}, bf16[24,1408]{1,0:T(8,128)(2,1)S(1)}, u32[]{:S(2)}, u32[]{:S(2)}) %collective-permute-start.4) | collective-permute-done | bytes 67616 | tf_op jit(solution)/shard_map/ppermute | solution.py:37
  25.2 2.1 %shard_map.150 = (bf16[24,1024]{1,0:T(8,128)(2,1)S(1)}, bf16[24,1024]{1,0:T(8,128)(2,1)S(1)}, bf16[24,1024]{1,0:T(8,128)(2,1)S(1)}, bf16[24,1024]{1,0:T(8,128)(2,1)S(1)}) custom-call(bf16[24,1408]{1,0:T(8,128)(2,1)S(1)} %get-tuple-element.64.refs_0_, bf16[24,1408]{1,0:T(8,128)(2,1)S(1)} %collective-permute-done.1.refs_1_, ...), custom_call_target="tpu_custom_call" | custom-call | flops 12582912 | bytes 2097152 | tf_op jit(solution)/shard_map/pallas_call | solution.py:23
  29.6 2.4 %collective-permute-done.6.refs_1_ = bf16[24,1024]{1,0:T(8,128)(2,1)S(1)} collective-permute-done((bf16[24,1024]{1,0:T(8,128)(2,1)S(1)}, bf16[24,1024]{1,0:T(8,128)(2,1)S(1)}, u32[]{:S(2)}, u32[]{:S(2)}) %collective-permute-start.6) | collective-permute-done | bytes 49184 | tf_op jit(solution)/shard_map/ppermute | solution.py:37
  32.9 3.4 %collective-permute-start.10 = (bf16[24,1024]{1,0:T(8,128)(2,1)S(1)}, bf16[24,1024]{1,0:T(8,128)(2,1)S(1)}, u32[]{:S(2)}, u32[]{:S(2)}) collective-permute-start(bf16[24,1024]{1,0:T(8,128)(2,1)S(1)} %get-tuple-element.86), channel_id=1, source_target_pairs={{0,3},{1,2},{2,1},{3,0},{4,7},{5,6},{6,5},{7,4},{8,11},{9,10},{10,... | collective-permute-start | bytes 147464 | tf_op jit(solution)/shard_map/ppermute | solution.py:37
  37.1 1.9 %collective-permute-done.10.refs_0_ = bf16[24,1024]{1,0:T(8,128)(2,1)S(1)} collective-permute-done((bf16[24,1024]{1,0:T(8,128)(2,1)S(1)}, bf16[24,1024]{1,0:T(8,128)(2,1)S(1)}, u32[]{:S(2)}, u32[]{:S(2)}) %collective-permute-start.10) | collective-permute-done | bytes 49184 | tf_op jit(solution)/shard_map/ppermute | solution.py:37
  39.1 3.1 %collective-permute-start.9 = (bf16[24,2048]{1,0:T(8,128)(2,1)S(1)}, bf16[24,2048]{1,0:T(8,128)(2,1)S(1)}, u32[]{:S(2)}, u32[]{:S(2)}) collective-permute-start(bf16[24,2048]{1,0:T(8,128)(2,1)S(1)} %shard_map.152), channel_id=1, source_target_pairs={{0,2},{1,3},{2,0},{3,1},{4,6},{5,7},{6,4},{7,5},{8,10},{9,11},{10,... | collective-permute-start | bytes 294920 | tf_op jit(solution)/shard_map/ppermute | solution.py:37
  43.8 2.0 %collective-permute-done.9.refs_2_ = bf16[24,2048]{1,0:T(8,128)(2,1)S(1)} collective-permute-done((bf16[24,2048]{1,0:T(8,128)(2,1)S(1)}, bf16[24,2048]{1,0:T(8,128)(2,1)S(1)}, u32[]{:S(2)}, u32[]{:S(2)}) %collective-permute-start.9) | collective-permute-done | bytes 98336 | tf_op jit(solution)/shard_map/ppermute | solution.py:37
  45.8 3.7 %collective-permute-done.11.refs_3_ = bf16[24,2048]{1,0:T(8,128)(2,1)S(1)} collective-permute-done((bf16[24,2048]{1,0:T(8,128)(2,1)S(1)}, bf16[24,2048]{1,0:T(8,128)(2,1)S(1)}, u32[]{:S(2)}, u32[]{:S(2)}) %collective-permute-start.11) | collective-permute-done | bytes 98336 | tf_op jit(solution)/shard_map/ppermute | solution.py:37
  49.7 3.4 %collective-permute-start.12 = (bf16[24,2048]{1,0:T(8,128)(2,1)S(1)}, bf16[24,2048]{1,0:T(8,128)(2,1)S(1)}, u32[]{:S(2)}, u32[]{:S(2)}) collective-permute-start(bf16[24,2048]{1,0:T(8,128)(2,1)S(1)} %get-tuple-element.87.refs_0_), channel_id=1, source_target_pairs={{0,1},{1,0},{2,3},{3,2},{4,5},{5,4},{6,7},{7,6},{8,9},{9,8},{10,11... | collective-permute-start | bytes 294920 | tf_op jit(solution)/shard_map/ppermute | solution.py:37
  55.7 2.7 %collective-permute-start.23 = (bf16[24,2048]{1,0:T(8,128)(2,1)S(1)}, bf16[24,2048]{1,0:T(8,128)(2,1)S(1)}, u32[]{:S(2)}, u32[]{:S(2)}) collective-permute-start(bf16[24,2048]{1,0:T(8,128)(2,1)S(1)} %get-tuple-element.87.refs_0_), channel_id=1, source_target_pairs={{0,3},{1,2},{2,1},{3,0},{4,7},{5,6},{6,5},{7,4},{8,11},{9,10},{10,... | collective-permute-start | bytes 294920 | tf_op jit(solution)/shard_map/ppermute | solution.py:37
  59.7 2.5 %collective-permute-done.23.refs_3_ = bf16[24,2048]{1,0:T(8,128)(2,1)S(1)} collective-permute-done((bf16[24,2048]{1,0:T(8,128)(2,1)S(1)}, bf16[24,2048]{1,0:T(8,128)(2,1)S(1)}, u32[]{:S(2)}, u32[]{:S(2)}) %collective-permute-start.23) | collective-permute-done | bytes 98336 | tf_op jit(solution)/shard_map/ppermute | solution.py:37
  65.6 2.2 %collective-permute-done.24.refs_1_ = bf16[32,2048]{1,0:T(8,128)(2,1)S(1)} collective-permute-done((bf16[32,2048]{1,0:T(8,128)(2,1)S(1)}, bf16[32,2048]{1,0:T(8,128)(2,1)S(1)}, u32[]{:S(2)}, u32[]{:S(2)}) %collective-permute-start.24) | collective-permute-done | bytes 131104 | tf_op jit(solution)/shard_map/ppermute | solution.py:37
  67.8 3.4 %collective-permute-start.26 = (bf16[32,2048]{1,0:T(8,128)(2,1)S(1)}, bf16[32,2048]{1,0:T(8,128)(2,1)S(1)}, u32[]{:S(2)}, u32[]{:S(2)}) collective-permute-start(bf16[32,2048]{1,0:T(8,128)(2,1)S(1)} %get-tuple-element.102), channel_id=1, source_target_pairs={{0,12},{4,8},{8,4},{12,0},{1,13},{5,9},{9,5},{13,1},{2,14},{6,10},... | collective-permute-start | bytes 393224 | tf_op jit(solution)/shard_map/ppermute | solution.py:37
  71.8 3.5 %collective-permute-done.26.refs_3_ = bf16[32,2048]{1,0:T(8,128)(2,1)S(1)} collective-permute-done((bf16[32,2048]{1,0:T(8,128)(2,1)S(1)}, bf16[32,2048]{1,0:T(8,128)(2,1)S(1)}, u32[]{:S(2)}, u32[]{:S(2)}) %collective-permute-start.26) | collective-permute-done | bytes 131104 | tf_op jit(solution)/shard_map/ppermute | solution.py:37
  78.2 2.0 %shard_map.159 = (bf16[32,2048]{1,0:T(8,128)(2,1)S(1)}, bf16[32,2048]{1,0:T(8,128)(2,1)S(1)}, bf16[32,2048]{1,0:T(8,128)(2,1)S(1)}, bf16[32,2048]{1,0:T(8,128)(2,1)S(1)}) custom-call(bf16[32,2048]{1,0:T(8,128)(2,1)S(1)} %get-tuple-element.99.refs_0_, bf16[32,2048]{1,0:T(8,128)(2,1)S(1)} %collective-permute-done.24.refs_1_, ...), custom_call_target="tpu_custom_call" | custom-call | flops 1207959552 | bytes 4194304 | tf_op jit(solution)/shard_map/pallas_call | solution.py:23
  91.0 2.3 %collective-permute-done.21.refs_3_ = bf16[24,2048]{1,0:T(8,128)(2,1)S(1)} collective-permute-done((bf16[24,2048]{1,0:T(8,128)(2,1)S(1)}, bf16[24,2048]{1,0:T(8,128)(2,1)S(1)}, u32[]{:S(2)}, u32[]{:S(2)}) %collective-permute-start.21) | collective-permute-done | bytes 98336 | tf_op jit(solution)/shard_map/ppermute | solution.py:37
  93.7 2.8 %collective-permute-start.32 = (bf16[24,2048]{1,0:T(8,128)(2,1)S(1)}, bf16[24,2048]{1,0:T(8,128)(2,1)S(1)}, u32[]{:S(2)}, u32[]{:S(2)}) collective-permute-start(bf16[24,2048]{1,0:T(8,128)(2,1)S(1)} %get-tuple-element.110), channel_id=1, source_target_pairs={{0,3},{1,2},{2,1},{3,0},{4,7},{5,6},{6,5},{7,4},{8,11},{9,10},{10,... | collective-permute-start | bytes 294920 | tf_op jit(solution)/shard_map/ppermute | solution.py:37
  98.2 2.0 %collective-permute-done.32.refs_3_ = bf16[24,2048]{1,0:T(8,128)(2,1)S(1)} collective-permute-done((bf16[24,2048]{1,0:T(8,128)(2,1)S(1)}, bf16[24,2048]{1,0:T(8,128)(2,1)S(1)}, u32[]{:S(2)}, u32[]{:S(2)}) %collective-permute-start.32) | collective-permute-done | bytes 98336 | tf_op jit(solution)/shard_map/ppermute | solution.py:37
  (89 shorter events, 36.5 us)
Async XLA Ops:
  0.0 76.7 %collective-permute-start.16 = (bf16[2048,384]{1,0:T(8,128)(2,1)}, bf16[2048,384]{1,0:T(8,128)(2,1)S(1)}, u32[]{:S(2)}, u32[]{:S(2)}) collective-permute-start(bf16[2048,384]{1,0:T(8,128)(2,1)} %bitcast.8), channel_id=1, source_target_pairs={{0,16},{16,0},{1,17},{17,1},{2,18},{18,2},{3,19},{19,3},{4,20},{20... | collective-permute-start | bytes 4718600 | tf_op jit(solution)/shard_map/ppermute | solution.py:307
  0.5 77.7 %collective-permute-start.17 = (bf16[2048,384]{1,0:T(8,128)(2,1)}, bf16[2048,384]{1,0:T(8,128)(2,1)S(1)}, u32[]{:S(2)}, u32[]{:S(2)}) collective-permute-start(bf16[2048,384]{1,0:T(8,128)(2,1)} %bitcast.11), channel_id=1, source_target_pairs={{0,16},{16,0},{1,17},{17,1},{2,18},{18,2},{3,19},{19,3},{4,20},{20... | collective-permute-start | bytes 4718600 | tf_op jit(solution)/shard_map/ppermute | solution.py:307
  0.5 77.6 %collective-permute-start.18 = (bf16[384,2048]{1,0:T(8,128)(2,1)}, bf16[384,2048]{1,0:T(8,128)(2,1)S(1)}, u32[]{:S(2)}, u32[]{:S(2)}) collective-permute-start(bf16[384,2048]{1,0:T(8,128)(2,1)} %bitcast.14), channel_id=1, source_target_pairs={{0,16},{16,0},{1,17},{17,1},{2,18},{18,2},{3,19},{19,3},{4,20},{20... | collective-permute-start | bytes 4718600 | tf_op jit(solution)/shard_map/ppermute | solution.py:307
  1.0 7.7 %collective-permute-start = (bf16[24,2048]{1,0:T(8,128)(2,1)}, bf16[24,2048]{1,0:T(8,128)(2,1)S(1)}, u32[]{:S(2)}, u32[]{:S(2)}) collective-permute-start(bf16[24,2048]{1,0:T(8,128)(2,1)} %refs_2_.2), channel_id=1, source_target_pairs={{0,1},{1,0},{2,3},{3,2},{4,5},{5,4},{6,7},{7,6},{8,9},{9,8},{10,11... | collective-permute-start | bytes 294920 | tf_op jit(solution)/shard_map/ppermute | solution.py:37
  3.6 9.7 %collective-permute-start.2 = (bf16[24,2048]{1,0:T(8,128)(2,1)}, bf16[24,2048]{1,0:T(8,128)(2,1)S(1)}, u32[]{:S(2)}, u32[]{:S(2)}) collective-permute-start(bf16[24,2048]{1,0:T(8,128)(2,1)} %refs_2_.2), channel_id=1, source_target_pairs={{0,2},{1,3},{2,0},{3,1},{4,6},{5,7},{6,4},{7,5},{8,10},{9,11},{10,... | collective-permute-start | bytes 294920 | tf_op jit(solution)/shard_map/ppermute | solution.py:37
  8.7 7.4 %collective-permute-start.3 = (bf16[24,2048]{1,0:T(8,128)(2,1)S(1)}, bf16[24,2048]{1,0:T(8,128)(2,1)S(1)}, u32[]{:S(2)}, u32[]{:S(2)}) collective-permute-start(bf16[24,2048]{1,0:T(8,128)(2,1)S(1)} %copy-done.10), channel_id=1, source_target_pairs={{0,3},{1,2},{2,1},{3,0},{4,7},{5,6},{6,5},{7,4},{8,11},{9,10},{10,... | collective-permute-start | bytes 294920 | tf_op jit(solution)/shard_map/ppermute | solution.py:37
  17.2 7.0 %collective-permute-start.4 = (bf16[24,1408]{1,0:T(8,128)(2,1)S(1)}, bf16[24,1408]{1,0:T(8,128)(2,1)S(1)}, u32[]{:S(2)}, u32[]{:S(2)}) collective-permute-start(bf16[24,1408]{1,0:T(8,128)(2,1)S(1)} %get-tuple-element.66), channel_id=1, source_target_pairs={{0,2},{1,3},{2,0},{3,1},{4,6},{5,7},{6,4},{7,5},{8,10},{9,11},{10,... | collective-permute-start | bytes 202760 | tf_op jit(solution)/shard_map/ppermute | solution.py:37
  17.9 7.3 %collective-permute-start.5 = (bf16[24,1408]{1,0:T(8,128)(2,1)S(1)}, bf16[24,1408]{1,0:T(8,128)(2,1)S(1)}, u32[]{:S(2)}, u32[]{:S(2)}) collective-permute-start(bf16[24,1408]{1,0:T(8,128)(2,1)S(1)} %get-tuple-element.67), channel_id=1, source_target_pairs={{0,3},{1,2},{2,1},{3,0},{4,7},{5,6},{6,5},{7,4},{8,11},{9,10},{10,... | collective-permute-start | bytes 202760 | tf_op jit(solution)/shard_map/ppermute | solution.py:37
  32.8 10.2 %collective-permute-start.7 = (bf16[24,2048]{1,0:T(8,128)(2,1)S(1)}, bf16[24,2048]{1,0:T(8,128)(2,1)S(1)}, u32[]{:S(2)}, u32[]{:S(2)}) collective-permute-start(bf16[24,2048]{1,0:T(8,128)(2,1)S(1)} %get-tuple-element.84), channel_id=1, source_target_pairs={{0,1},{1,0},{2,3},{3,2},{4,5},{5,4},{6,7},{7,6},{8,9},{9,8},{10,11... | collective-permute-start | bytes 294920 | tf_op jit(solution)/shard_map/ppermute | solution.py:37
  32.9 6.2 %collective-permute-start.10 = (bf16[24,1024]{1,0:T(8,128)(2,1)S(1)}, bf16[24,1024]{1,0:T(8,128)(2,1)S(1)}, u32[]{:S(2)}, u32[]{:S(2)}) collective-permute-start(bf16[24,1024]{1,0:T(8,128)(2,1)S(1)} %get-tuple-element.86), channel_id=1, source_target_pairs={{0,3},{1,2},{2,1},{3,0},{4,7},{5,6},{6,5},{7,4},{8,11},{9,10},{10,... | collective-permute-start | bytes 147464 | tf_op jit(solution)/shard_map/ppermute | solution.py:37
  39.1 6.8 %collective-permute-start.9 = (bf16[24,2048]{1,0:T(8,128)(2,1)S(1)}, bf16[24,2048]{1,0:T(8,128)(2,1)S(1)}, u32[]{:S(2)}, u32[]{:S(2)}) collective-permute-start(bf16[24,2048]{1,0:T(8,128)(2,1)S(1)} %shard_map.152), channel_id=1, source_target_pairs={{0,2},{1,3},{2,0},{3,1},{4,6},{5,7},{6,4},{7,5},{8,10},{9,11},{10,... | collective-permute-start | bytes 294920 | tf_op jit(solution)/shard_map/ppermute | solution.py:37
  43.0 6.5 %collective-permute-start.11 = (bf16[24,2048]{1,0:T(8,128)(2,1)S(1)}, bf16[24,2048]{1,0:T(8,128)(2,1)S(1)}, u32[]{:S(2)}, u32[]{:S(2)}) collective-permute-start(bf16[24,2048]{1,0:T(8,128)(2,1)S(1)} %shard_map.153), channel_id=1, source_target_pairs={{0,3},{1,2},{2,1},{3,0},{4,7},{5,6},{6,5},{7,4},{8,11},{9,10},{10,... | collective-permute-start | bytes 294920 | tf_op jit(solution)/shard_map/ppermute | solution.py:37
  53.1 6.6 %collective-permute-start.22 = (bf16[24,2048]{1,0:T(8,128)(2,1)S(1)}, bf16[24,2048]{1,0:T(8,128)(2,1)S(1)}, u32[]{:S(2)}, u32[]{:S(2)}) collective-permute-start(bf16[24,2048]{1,0:T(8,128)(2,1)S(1)} %get-tuple-element.87.refs_0_), channel_id=1, source_target_pairs={{0,2},{1,3},{2,0},{3,1},{4,6},{5,7},{6,4},{7,5},{8,10},{9,11},{10,... | collective-permute-start | bytes 294920 | tf_op jit(solution)/shard_map/ppermute | solution.py:37
  55.7 6.5 %collective-permute-start.23 = (bf16[24,2048]{1,0:T(8,128)(2,1)S(1)}, bf16[24,2048]{1,0:T(8,128)(2,1)S(1)}, u32[]{:S(2)}, u32[]{:S(2)}) collective-permute-start(bf16[24,2048]{1,0:T(8,128)(2,1)S(1)} %get-tuple-element.87.refs_0_), channel_id=1, source_target_pairs={{0,3},{1,2},{2,1},{3,0},{4,7},{5,6},{6,5},{7,4},{8,11},{9,10},{10,... | collective-permute-start | bytes 294920 | tf_op jit(solution)/shard_map/ppermute | solution.py:37
  64.1 7.7 %collective-permute-start.25 = (bf16[32,2048]{1,0:T(8,128)(2,1)S(1)}, bf16[32,2048]{1,0:T(8,128)(2,1)S(1)}, u32[]{:S(2)}, u32[]{:S(2)}) collective-permute-start(bf16[32,2048]{1,0:T(8,128)(2,1)S(1)} %get-tuple-element.101), channel_id=1, source_target_pairs={{0,8},{4,12},{8,0},{12,4},{1,9},{5,13},{9,1},{13,5},{2,10},{6,14},... | collective-permute-start | bytes 393224 | tf_op jit(solution)/shard_map/ppermute | solution.py:37
  67.8 7.6 %collective-permute-start.26 = (bf16[32,2048]{1,0:T(8,128)(2,1)S(1)}, bf16[32,2048]{1,0:T(8,128)(2,1)S(1)}, u32[]{:S(2)}, u32[]{:S(2)}) collective-permute-start(bf16[32,2048]{1,0:T(8,128)(2,1)S(1)} %get-tuple-element.102), channel_id=1, source_target_pairs={{0,12},{4,8},{8,4},{12,0},{1,13},{5,9},{9,5},{13,1},{2,14},{6,10},... | collective-permute-start | bytes 393224 | tf_op jit(solution)/shard_map/ppermute | solution.py:37
  71.8 10.5 %collective-permute-start.13 = (bf16[24,2048]{1,0:T(8,128)(2,1)S(1)}, bf16[24,2048]{1,0:T(8,128)(2,1)S(1)}, u32[]{:S(2)}, u32[]{:S(2)}) collective-permute-start(bf16[24,2048]{1,0:T(8,128)(2,1)S(1)} %get-tuple-element.91), channel_id=1, source_target_pairs={{0,4},{4,0},{8,12},{12,8},{1,5},{5,1},{9,13},{13,9},{2,6},{6,2},{1... | collective-permute-start | bytes 294920 | tf_op jit(solution)/shard_map/ppermute | solution.py:37
  75.4 8.3 %collective-permute-start.14 = (bf16[24,2048]{1,0:T(8,128)(2,1)S(1)}, bf16[24,2048]{1,0:T(8,128)(2,1)S(1)}, u32[]{:S(2)}, u32[]{:S(2)}) collective-permute-start(bf16[24,2048]{1,0:T(8,128)(2,1)S(1)} %get-tuple-element.92), channel_id=1, source_target_pairs={{0,8},{4,12},{8,0},{12,4},{1,9},{5,13},{9,1},{13,5},{2,10},{6,14},... | collective-permute-start | bytes 294920 | tf_op jit(solution)/shard_map/ppermute | solution.py:37
  76.7 7.0 %collective-permute-start.15 = (bf16[24,2048]{1,0:T(8,128)(2,1)S(1)}, bf16[24,2048]{1,0:T(8,128)(2,1)S(1)}, u32[]{:S(2)}, u32[]{:S(2)}) collective-permute-start(bf16[24,2048]{1,0:T(8,128)(2,1)S(1)} %get-tuple-element.93), channel_id=1, source_target_pairs={{0,12},{4,8},{8,4},{12,0},{1,13},{5,9},{9,5},{13,1},{2,14},{6,10},... | collective-permute-start | bytes 294920 | tf_op jit(solution)/shard_map/ppermute | solution.py:37
  80.1 7.6 %collective-permute-start.27 = (bf16[32,2048]{1,0:T(8,128)(2,1)S(1)}, bf16[32,2048]{1,0:T(8,128)(2,1)S(1)}, u32[]{:S(2)}, u32[]{:S(2)}) collective-permute-start(bf16[32,2048]{1,0:T(8,128)(2,1)S(1)} %get-tuple-element.104), channel_id=1, source_target_pairs={{0,4},{4,0},{8,12},{12,8},{1,5},{5,1},{9,13},{13,9},{2,6},{6,2},{1... | collective-permute-start | bytes 393224 | tf_op jit(solution)/shard_map/ppermute | solution.py:37
  80.9 8.2 %collective-permute-start.28 = (bf16[32,2048]{1,0:T(8,128)(2,1)S(1)}, bf16[32,2048]{1,0:T(8,128)(2,1)S(1)}, u32[]{:S(2)}, u32[]{:S(2)}) collective-permute-start(bf16[32,2048]{1,0:T(8,128)(2,1)S(1)} %get-tuple-element.105), channel_id=1, source_target_pairs={{0,8},{4,12},{8,0},{12,4},{1,9},{5,13},{9,1},{13,5},{2,10},{6,14},... | collective-permute-start | bytes 393224 | tf_op jit(solution)/shard_map/ppermute | solution.py:37
  82.3 6.8 %collective-permute-start.29 = (bf16[32,2048]{1,0:T(8,128)(2,1)S(1)}, bf16[32,2048]{1,0:T(8,128)(2,1)S(1)}, u32[]{:S(2)}, u32[]{:S(2)}) collective-permute-start(bf16[32,2048]{1,0:T(8,128)(2,1)S(1)} %get-tuple-element.106), channel_id=1, source_target_pairs={{0,12},{4,8},{8,4},{12,0},{1,13},{5,9},{9,5},{13,1},{2,14},{6,10},... | collective-permute-start | bytes 393224 | tf_op jit(solution)/shard_map/ppermute | solution.py:37
  89.3 8.9 %collective-permute-start.31 = (bf16[24,2048]{1,0:T(8,128)(2,1)S(1)}, bf16[24,2048]{1,0:T(8,128)(2,1)S(1)}, u32[]{:S(2)}, u32[]{:S(2)}) collective-permute-start(bf16[24,2048]{1,0:T(8,128)(2,1)S(1)} %get-tuple-element.107.refs_10_), channel_id=1, source_target_pairs={{0,2},{1,3},{2,0},{3,1},{4,6},{5,7},{6,4},{7,5},{8,10},{9,11},{10,... | collective-permute-start | bytes 294920 | tf_op jit(solution)/shard_map/ppermute | solution.py:37
  93.7 6.5 %collective-permute-start.32 = (bf16[24,2048]{1,0:T(8,128)(2,1)S(1)}, bf16[24,2048]{1,0:T(8,128)(2,1)S(1)}, u32[]{:S(2)}, u32[]{:S(2)}) collective-permute-start(bf16[24,2048]{1,0:T(8,128)(2,1)S(1)} %get-tuple-element.110), channel_id=1, source_target_pairs={{0,3},{1,2},{2,1},{3,0},{4,7},{5,6},{6,5},{7,4},{8,11},{9,10},{10,... | collective-permute-start | bytes 294920 | tf_op jit(solution)/shard_map/ppermute | solution.py:37
  (21 other events, 209.5 us)

commit v3 on v2

--- a/solution.py
+++ b/solution.py
@@ -129,22 +129,23 @@
             out[...] = jnp.broadcast_to(value, out.shape)
 
 
-def mix_kernel(count, done, *refs):
+def mix_kernel(count, done, steps, *refs):
     messages, parts = refs[:count], refs[count : count + 4 * done]
     refs = refs[count + 4 * done :]
     q_gain, k_gain, cosine, sine, bias, keys, values = refs[:7]
-    outs = refs[7 : 7 + count]
-    scratch, k_rot, v_new, kv_all = refs[7 + count :]
+    outs = refs[7 : 7 + len(steps)]
+    scratch, k_rot, v_new, kv_all = refs[7 + len(steps) :]
     me = lax.axis_index("dev")
     rows, heads, _, dim = keys.shape
     group = scratch.shape[1] // rows
     query_width = group * dim
     kv_width = kv_all.shape[2]
     cos, sin = cosine[...], sine[...]
-    last = [
-        attend_cache(messages[step], me ^ step, q_gain[...], cos, sin, bias[...], keys, values, scratch.at[step])
-        for step in range(done, count)
-    ]
+    last = {
+        step: attend_cache(messages[step], me ^ step, q_gain[...], cos, sin, bias[...], keys, values, scratch.at[step])
+        for step in steps
+        if step >= done
+    }
     for step in range(count):
         kv_all[me ^ step] = messages[step][:, query_width : query_width + kv_width].astype(F32)
     for h in range(2 * heads):
@@ -154,22 +155,22 @@
             k_rot[h] = turn(piece, k_gain[...], cos, sin).astype(BF16).astype(F32)
         else:
             v_new[h - heads] = piece
-    for step in reversed(range(count)):
+    for out, step in reversed(list(zip(outs, steps))):
         head = me ^ step
         if step < done:
             query, top, total, mixed = [ref[...] for ref in parts[4 * step : 4 * step + 4]]
             top, total = top[:, :, :1], total[:, :, :1]
         else:
-            query, top, total, mixed = last[step - done]
+            query, top, total, mixed = last[step]
         new = jnp.sum(query * k_rot[head][:, None, :], axis=-1, keepdims=True) * dim ** (-0.5)
         highest = jnp.maximum(top, new)
         old = jnp.exp(top - highest)
         new = jnp.exp(new - highest)
         share = 1.0 / (total * old + new)
-        out = mixed * (old * share) + (new * share) * v_new[head][:, None, :]
-        scratch[step] = out.reshape(rows * group, dim)
+        found = mixed * (old * share) + (new * share) * v_new[head][:, None, :]
+        scratch[step] = found.reshape(rows * group, dim)
         for h in range(group):
-            outs[step][:, h * dim : (h + 1) * dim] = scratch[step, pl.ds(h, rows, stride=group), :].astype(BF16)
+            out[:, h * dim : (h + 1) * dim] = scratch[step, pl.ds(h, rows, stride=group), :].astype(BF16)
 
 
 def out_kernel(count, *refs):
@@ -345,20 +346,24 @@
             cost=(len(chunk) * flops, 2 << 20),
             limit=4 << 20,
         )
-    mixtures = call(
-        functools.partial(mix_kernel, count, count - 1),
-        [((rows, query_width), BF16)] * count,
-        [VMEM] * (count + 4 * (count - 1) + 7),
-        [*messages, *parts, *gains, cosine, sine, bias, cache_keys, cache_values],
-        scratch=[
-            pltpu.VMEM((count, rows * group, dim), F32),
-            pltpu.VMEM((heads, rows, dim), F32),
-            pltpu.VMEM((heads, rows, dim), F32),
-            pltpu.VMEM((count, rows, kv_width), F32),
-        ],
-        cost=(flops, 2 << 20),
-        limit=4 << 20,
-    )
+    mixtures = [None] * count
+    for steps in ([1], [0, *range(2, count)]):
+        made = call(
+            functools.partial(mix_kernel, count, count - 1, steps),
+            [((rows, query_width), BF16)] * len(steps),
+            [VMEM] * (count + 4 * (count - 1) + 7),
+            [*messages, *parts, *gains, cosine, sine, bias, cache_keys, cache_values],
+            scratch=[
+                pltpu.VMEM((count, rows * group, dim), F32),
+                pltpu.VMEM((heads, rows, dim), F32),
+                pltpu.VMEM((heads, rows, dim), F32),
+                pltpu.VMEM((count, rows, kv_width), F32),
+            ],
+            cost=(flops, 2 << 20),
+            limit=4 << 20,
+        )
+        for step, mixture in zip(steps, made):
+            mixtures[step] = mixture
     choices = call(
         functools.partial(route_kernel, count, groups, capacity),
         [((half * rows, groups * strides[0]), BF16), ((count * rows, groups * strides[1]), BF16)],

time: 101 us -> 99.5 us (0.985)
  starting transfers between devices: 50.6 us -> 44.5 us
  waiting for transfers between devices: 31.7 us -> 36.4 us
    ppermute x30, starting transfers between devices: 49.6 us -> 43.5 us  [exchange(): lax.ppermute(pieces[step], axis, [(i, i ^ step) for i in range(size)])]
    ppermute x30, waiting for transfers between devices: 31.7 us -> 36.4 us  [exchange(): lax.ppermute(pieces[step], axis, [(i, i ^ step) for i in range(size)])]
    pallas_call x18 -> x19, Pallas kernels: 17.9 us -> 17.8 us  [call(): pl.pallas_call(kernel, out_shape=[place(shape, dtype) for shape, dtype in...]
  transfers between devices with their start and end apart: 33 -> 33, of which waited for: 15 -> 17; matrix products, arithmetic and copies ran while one was open for 0% -> 0% of each run, Pallas kernels for 17% -> 17%
where the time goes in v3:
time: 99.5 us; the launch traced here: 99.3 us
  starting transfers between devices  44.5 us (45%)
  waiting for transfers between devices  36.4 us (37%)
  Pallas kernels  17.8 us (18%)
    ppermute x30, starting transfers between devices, exchange(): lax.ppermute(pieces[step], axis, [(i, i ^ step) for i in range(size)])  43.5 us
    ppermute x30, waiting for transfers between devices, exchange(): lax.ppermute(pieces[step], axis, [(i, i ^ step) for i in range(size)])  36.4 us
    pallas_call x19, Pallas kernels, call(): pl.pallas_call(kernel, out_shape=[place(shape, dtype) for shape, dtype in...  17.8 us
  transfers between devices with their start and end apart: 33, of which 17 were waited for; matrix products, arithmetic and copies ran while one was open for 0% of the time, Pallas kernels for 17%

profile of v3, /device:TPU:0, one launch (start us, length us, event | category | flops | bytes accessed | tf_op | source)
XLA Modules:
  0.0 99.3 jit_solution(956656544146678180)
XLA Ops:
  1.0 2.6 %collective-permute-start = (bf16[24,2048]{1,0:T(8,128)(2,1)}, bf16[24,2048]{1,0:T(8,128)(2,1)S(1)}, u32[]{:S(2)}, u32[]{:S(2)}) collective-permute-start(bf16[24,2048]{1,0:T(8,128)(2,1)} %refs_2_.2), channel_id=1, source_target_pairs={{0,1},{1,0},{2,3},{3,2},{4,5},{5,4},{6,7},{7,6},{8,9},{9,8},{10,11... | collective-permute-start | bytes 294920 | tf_op jit(solution)/shard_map/ppermute | solution.py:37
  3.6 2.6 %collective-permute-start.2 = (bf16[24,2048]{1,0:T(8,128)(2,1)}, bf16[24,2048]{1,0:T(8,128)(2,1)S(1)}, u32[]{:S(2)}, u32[]{:S(2)}) collective-permute-start(bf16[24,2048]{1,0:T(8,128)(2,1)} %refs_2_.2), channel_id=1, source_target_pairs={{0,2},{1,3},{2,0},{3,1},{4,6},{5,7},{6,4},{7,5},{8,10},{9,11},{10,... | collective-permute-start | bytes 294920 | tf_op jit(solution)/shard_map/ppermute | solution.py:37
  6.2 2.6 %shard_map.145 = (bf16[2048,1024]{1,0:T(8,128)(2,1)S(1)}, bf16[2048,256]{1,0:T(8,128)(2,1)S(1)}, bf16[24,2048]{1,0:T(8,128)(2,1)S(1)}, f32[1,2048]{1,0:T(1,128)S(1)}) custom-call(bf16[2048,1024]{1,0:T(8,128)(2,1)} %refs_0_.1, bf16[2048,256]{1,0:T(8,128)(2,1)} %refs_1_.3, bf16[24,2048]{1,0:T(8,128)(2,1)} %refs_2_.2, f32[1,2048]{1,0:T(1,128)} %bitcast.26), custom_call_target="tpu_custom_call" | custom-call | bytes 5349376 | tf_op jit(solution)/shard_map/pallas_call | solution.py:23
  8.7 3.3 %collective-permute-start.3 = (bf16[24,2048]{1,0:T(8,128)(2,1)S(1)}, bf16[24,2048]{1,0:T(8,128)(2,1)S(1)}, u32[]{:S(2)}, u32[]{:S(2)}) collective-permute-start(bf16[24,2048]{1,0:T(8,128)(2,1)S(1)} %copy-done.10), channel_id=1, source_target_pairs={{0,3},{1,2},{2,1},{3,0},{4,7},{5,6},{6,5},{7,4},{8,11},{9,10},{10,... | collective-permute-start | bytes 294920 | tf_op jit(solution)/shard_map/ppermute | solution.py:37
  13.4 2.8 %collective-permute-done.3.refs_1_ = bf16[24,2048]{1,0:T(8,128)(2,1)S(1)} collective-permute-done((bf16[24,2048]{1,0:T(8,128)(2,1)S(1)}, bf16[24,2048]{1,0:T(8,128)(2,1)S(1)}, u32[]{:S(2)}, u32[]{:S(2)}) %collective-permute-start.3) | collective-permute-done | bytes 98336 | tf_op jit(solution)/shard_map/ppermute | solution.py:37
  17.9 2.7 %collective-permute-start.5 = (bf16[24,1408]{1,0:T(8,128)(2,1)S(1)}, bf16[24,1408]{1,0:T(8,128)(2,1)S(1)}, u32[]{:S(2)}, u32[]{:S(2)}) collective-permute-start(bf16[24,1408]{1,0:T(8,128)(2,1)S(1)} %get-tuple-element.66), channel_id=1, source_target_pairs={{0,3},{1,2},{2,1},{3,0},{4,7},{5,6},{6,5},{7,4},{8,11},{9,10},{10,... | collective-permute-start | bytes 202760 | tf_op jit(solution)/shard_map/ppermute | solution.py:37
  22.2 2.1 %collective-permute-done.4.refs_0_.refs_2_ = bf16[24,1408]{1,0:T(8,128)(2,1)S(1)} collective-permute-done((bf16[24,1408]{1,0:T(8,128)(2,1)S(1)}, bf16[24,1408]{1,0:T(8,128)(2,1)S(1)}, u32[]{:S(2)}, u32[]{:S(2)}) %collective-permute-start.4) | collective-permute-done | bytes 67616 | tf_op jit(solution)/shard_map/ppermute | solution.py:37
  27.7 1.9 %collective-permute-start.8 = (bf16[24,1024]{1,0:T(8,128)(2,1)S(1)}, bf16[24,1024]{1,0:T(8,128)(2,1)S(1)}, u32[]{:S(2)}, u32[]{:S(2)}) collective-permute-start(bf16[24,1024]{1,0:T(8,128)(2,1)S(1)} %get-tuple-element.83), channel_id=1, source_target_pairs={{0,2},{1,3},{2,0},{3,1},{4,6},{5,7},{6,4},{7,5},{8,10},{9,11},{10,... | collective-permute-start | bytes 147464 | tf_op jit(solution)/shard_map/ppermute | solution.py:37
  32.9 2.1 %collective-permute-start.10 = (bf16[24,1024]{1,0:T(8,128)(2,1)S(1)}, bf16[24,1024]{1,0:T(8,128)(2,1)S(1)}, u32[]{:S(2)}, u32[]{:S(2)}) collective-permute-start(bf16[24,1024]{1,0:T(8,128)(2,1)S(1)} %get-tuple-element.84), channel_id=1, source_target_pairs={{0,3},{1,2},{2,1},{3,0},{4,7},{5,6},{6,5},{7,4},{8,11},{9,10},{10,... | collective-permute-start | bytes 147464 | tf_op jit(solution)/shard_map/ppermute | solution.py:37
  35.8 3.0 %collective-permute-done.10.refs_0_ = bf16[24,1024]{1,0:T(8,128)(2,1)S(1)} collective-permute-done((bf16[24,1024]{1,0:T(8,128)(2,1)S(1)}, bf16[24,1024]{1,0:T(8,128)(2,1)S(1)}, u32[]{:S(2)}, u32[]{:S(2)}) %collective-permute-start.10) | collective-permute-done | bytes 49184 | tf_op jit(solution)/shard_map/ppermute | solution.py:37
  38.7 3.1 %collective-permute-start.9 = (bf16[24,2048]{1,0:T(8,128)(2,1)S(1)}, bf16[24,2048]{1,0:T(8,128)(2,1)S(1)}, u32[]{:S(2)}, u32[]{:S(2)}) collective-permute-start(bf16[24,2048]{1,0:T(8,128)(2,1)S(1)} %shard_map.153), channel_id=1, source_target_pairs={{0,2},{1,3},{2,0},{3,1},{4,6},{5,7},{6,4},{7,5},{8,10},{9,11},{10,... | collective-permute-start | bytes 294920 | tf_op jit(solution)/shard_map/ppermute | solution.py:37
  43.1 2.5 %collective-permute-done.9.refs_2_ = bf16[24,2048]{1,0:T(8,128)(2,1)S(1)} collective-permute-done((bf16[24,2048]{1,0:T(8,128)(2,1)S(1)}, bf16[24,2048]{1,0:T(8,128)(2,1)S(1)}, u32[]{:S(2)}, u32[]{:S(2)}) %collective-permute-start.9) | collective-permute-done | bytes 98336 | tf_op jit(solution)/shard_map/ppermute | solution.py:37
  45.6 3.6 %collective-permute-done.11.refs_3_ = bf16[24,2048]{1,0:T(8,128)(2,1)S(1)} collective-permute-done((bf16[24,2048]{1,0:T(8,128)(2,1)S(1)}, bf16[24,2048]{1,0:T(8,128)(2,1)S(1)}, u32[]{:S(2)}, u32[]{:S(2)}) %collective-permute-start.11) | collective-permute-done | bytes 98336 | tf_op jit(solution)/shard_map/ppermute | solution.py:37
  52.1 1.9 %collective-permute-done.12.refs_1_ = bf16[24,2048]{1,0:T(8,128)(2,1)S(1)} collective-permute-done((bf16[24,2048]{1,0:T(8,128)(2,1)S(1)}, bf16[24,2048]{1,0:T(8,128)(2,1)S(1)}, u32[]{:S(2)}, u32[]{:S(2)}) %collective-permute-start.12) | collective-permute-done | bytes 98336 | tf_op jit(solution)/shard_map/ppermute | solution.py:37
  54.0 2.1 %collective-permute-start.23 = (bf16[24,2048]{1,0:T(8,128)(2,1)S(1)}, bf16[24,2048]{1,0:T(8,128)(2,1)S(1)}, u32[]{:S(2)}, u32[]{:S(2)}) collective-permute-start(bf16[24,2048]{1,0:T(8,128)(2,1)S(1)} %get-tuple-element.85.refs_0_), channel_id=1, source_target_pairs={{0,3},{1,2},{2,1},{3,0},{4,7},{5,6},{6,5},{7,4},{8,11},{9,10},{10,... | collective-permute-start | bytes 294920 | tf_op jit(solution)/shard_map/ppermute | solution.py:37
  57.4 3.1 %collective-permute-done.23.refs_3_ = bf16[24,2048]{1,0:T(8,128)(2,1)S(1)} collective-permute-done((bf16[24,2048]{1,0:T(8,128)(2,1)S(1)}, bf16[24,2048]{1,0:T(8,128)(2,1)S(1)}, u32[]{:S(2)}, u32[]{:S(2)}) %collective-permute-start.23) | collective-permute-done | bytes 98336 | tf_op jit(solution)/shard_map/ppermute | solution.py:37
  63.9 3.0 %collective-permute-done.24.refs_1_ = bf16[32,2048]{1,0:T(8,128)(2,1)S(1)} collective-permute-done((bf16[32,2048]{1,0:T(8,128)(2,1)S(1)}, bf16[32,2048]{1,0:T(8,128)(2,1)S(1)}, u32[]{:S(2)}, u32[]{:S(2)}) %collective-permute-start.24) | collective-permute-done | bytes 131104 | tf_op jit(solution)/shard_map/ppermute | solution.py:37
  66.9 2.5 %collective-permute-start.26 = (bf16[32,2048]{1,0:T(8,128)(2,1)S(1)}, bf16[32,2048]{1,0:T(8,128)(2,1)S(1)}, u32[]{:S(2)}, u32[]{:S(2)}) collective-permute-start(bf16[32,2048]{1,0:T(8,128)(2,1)S(1)} %get-tuple-element.100), channel_id=1, source_target_pairs={{0,12},{4,8},{8,4},{12,0},{1,13},{5,9},{9,5},{13,1},{2,14},{6,10},... | collective-permute-start | bytes 393224 | tf_op jit(solution)/shard_map/ppermute | solution.py:37
  69.8 3.3 %collective-permute-done.26.refs_3_ = bf16[32,2048]{1,0:T(8,128)(2,1)S(1)} collective-permute-done((bf16[32,2048]{1,0:T(8,128)(2,1)S(1)}, bf16[32,2048]{1,0:T(8,128)(2,1)S(1)}, u32[]{:S(2)}, u32[]{:S(2)}) %collective-permute-start.26) | collective-permute-done | bytes 131104 | tf_op jit(solution)/shard_map/ppermute | solution.py:37
  76.6 2.0 %shard_map.160 = (bf16[32,2048]{1,0:T(8,128)(2,1)S(1)}, bf16[32,2048]{1,0:T(8,128)(2,1)S(1)}, bf16[32,2048]{1,0:T(8,128)(2,1)S(1)}, bf16[32,2048]{1,0:T(8,128)(2,1)S(1)}) custom-call(bf16[32,2048]{1,0:T(8,128)(2,1)S(1)} %get-tuple-element.97.refs_0_, bf16[32,2048]{1,0:T(8,128)(2,1)S(1)} %collective-permute-done.24.refs_1_, ...), custom_call_target="tpu_custom_call" | custom-call | flops 1207959552 | bytes 4194304 | tf_op jit(solution)/shard_map/pallas_call | solution.py:23
  89.2 2.4 %collective-permute-done.21.refs_3_ = bf16[24,2048]{1,0:T(8,128)(2,1)S(1)} collective-permute-done((bf16[24,2048]{1,0:T(8,128)(2,1)S(1)}, bf16[24,2048]{1,0:T(8,128)(2,1)S(1)}, u32[]{:S(2)}, u32[]{:S(2)}) %collective-permute-start.21) | collective-permute-done | bytes 98336 | tf_op jit(solution)/shard_map/ppermute | solution.py:37
  92.1 2.1 %collective-permute-start.32 = (bf16[24,2048]{1,0:T(8,128)(2,1)S(1)}, bf16[24,2048]{1,0:T(8,128)(2,1)S(1)}, u32[]{:S(2)}, u32[]{:S(2)}) collective-permute-start(bf16[24,2048]{1,0:T(8,128)(2,1)S(1)} %get-tuple-element.108), channel_id=1, source_target_pairs={{0,3},{1,2},{2,1},{3,0},{4,7},{5,6},{6,5},{7,4},{8,11},{9,10},{10,... | collective-permute-start | bytes 294920 | tf_op jit(solution)/shard_map/ppermute | solution.py:37
  94.2 2.4 %collective-permute-done.30.refs_1_ = bf16[24,2048]{1,0:T(8,128)(2,1)S(1)} collective-permute-done((bf16[24,2048]{1,0:T(8,128)(2,1)S(1)}, bf16[24,2048]{1,0:T(8,128)(2,1)S(1)}, u32[]{:S(2)}, u32[]{:S(2)}) %collective-permute-start.30) | collective-permute-done | bytes 98336 | tf_op jit(solution)/shard_map/ppermute | solution.py:37
  96.6 2.0 %collective-permute-done.32.refs_3_ = bf16[24,2048]{1,0:T(8,128)(2,1)S(1)} collective-permute-done((bf16[24,2048]{1,0:T(8,128)(2,1)S(1)}, bf16[24,2048]{1,0:T(8,128)(2,1)S(1)}, u32[]{:S(2)}, u32[]{:S(2)}) %collective-permute-start.32) | collective-permute-done | bytes 98336 | tf_op jit(solution)/shard_map/ppermute | solution.py:37
  (90 shorter events, 37.5 us)
Async XLA Ops:
  0.0 74.7 %collective-permute-start.16 = (bf16[2048,384]{1,0:T(8,128)(2,1)}, bf16[2048,384]{1,0:T(8,128)(2,1)S(1)}, u32[]{:S(2)}, u32[]{:S(2)}) collective-permute-start(bf16[2048,384]{1,0:T(8,128)(2,1)} %bitcast.8), channel_id=1, source_target_pairs={{0,16},{16,0},{1,17},{17,1},{2,18},{18,2},{3,19},{19,3},{4,20},{20... | collective-permute-start | bytes 4718600 | tf_op jit(solution)/shard_map/ppermute | solution.py:308
  0.5 76.1 %collective-permute-start.17 = (bf16[2048,384]{1,0:T(8,128)(2,1)}, bf16[2048,384]{1,0:T(8,128)(2,1)S(1)}, u32[]{:S(2)}, u32[]{:S(2)}) collective-permute-start(bf16[2048,384]{1,0:T(8,128)(2,1)} %bitcast.11), channel_id=1, source_target_pairs={{0,16},{16,0},{1,17},{17,1},{2,18},{18,2},{3,19},{19,3},{4,20},{20... | collective-permute-start | bytes 4718600 | tf_op jit(solution)/shard_map/ppermute | solution.py:308
  0.5 76.0 %collective-permute-start.18 = (bf16[384,2048]{1,0:T(8,128)(2,1)}, bf16[384,2048]{1,0:T(8,128)(2,1)S(1)}, u32[]{:S(2)}, u32[]{:S(2)}) collective-permute-start(bf16[384,2048]{1,0:T(8,128)(2,1)} %bitcast.14), channel_id=1, source_target_pairs={{0,16},{16,0},{1,17},{17,1},{2,18},{18,2},{3,19},{19,3},{4,20},{20... | collective-permute-start | bytes 4718600 | tf_op jit(solution)/shard_map/ppermute | solution.py:308
  1.0 7.7 %collective-permute-start = (bf16[24,2048]{1,0:T(8,128)(2,1)}, bf16[24,2048]{1,0:T(8,128)(2,1)S(1)}, u32[]{:S(2)}, u32[]{:S(2)}) collective-permute-start(bf16[24,2048]{1,0:T(8,128)(2,1)} %refs_2_.2), channel_id=1, source_target_pairs={{0,1},{1,0},{2,3},{3,2},{4,5},{5,4},{6,7},{7,6},{8,9},{9,8},{10,11... | collective-permute-start | bytes 294920 | tf_op jit(solution)/shard_map/ppermute | solution.py:37
  3.6 9.7 %collective-permute-start.2 = (bf16[24,2048]{1,0:T(8,128)(2,1)}, bf16[24,2048]{1,0:T(8,128)(2,1)S(1)}, u32[]{:S(2)}, u32[]{:S(2)}) collective-permute-start(bf16[24,2048]{1,0:T(8,128)(2,1)} %refs_2_.2), channel_id=1, source_target_pairs={{0,2},{1,3},{2,0},{3,1},{4,6},{5,7},{6,4},{7,5},{8,10},{9,11},{10,... | collective-permute-start | bytes 294920 | tf_op jit(solution)/shard_map/ppermute | solution.py:37
  8.7 7.4 %collective-permute-start.3 = (bf16[24,2048]{1,0:T(8,128)(2,1)S(1)}, bf16[24,2048]{1,0:T(8,128)(2,1)S(1)}, u32[]{:S(2)}, u32[]{:S(2)}) collective-permute-start(bf16[24,2048]{1,0:T(8,128)(2,1)S(1)} %copy-done.10), channel_id=1, source_target_pairs={{0,3},{1,2},{2,1},{3,0},{4,7},{5,6},{6,5},{7,4},{8,11},{9,10},{10,... | collective-permute-start | bytes 294920 | tf_op jit(solution)/shard_map/ppermute | solution.py:37
  17.3 7.0 %collective-permute-start.4 = (bf16[24,1408]{1,0:T(8,128)(2,1)S(1)}, bf16[24,1408]{1,0:T(8,128)(2,1)S(1)}, u32[]{:S(2)}, u32[]{:S(2)}) collective-permute-start(bf16[24,1408]{1,0:T(8,128)(2,1)S(1)} %get-tuple-element.65), channel_id=1, source_target_pairs={{0,2},{1,3},{2,0},{3,1},{4,6},{5,7},{6,4},{7,5},{8,10},{9,11},{10,... | collective-permute-start | bytes 202760 | tf_op jit(solution)/shard_map/ppermute | solution.py:37
  17.9 7.3 %collective-permute-start.5 = (bf16[24,1408]{1,0:T(8,128)(2,1)S(1)}, bf16[24,1408]{1,0:T(8,128)(2,1)S(1)}, u32[]{:S(2)}, u32[]{:S(2)}) collective-permute-start(bf16[24,1408]{1,0:T(8,128)(2,1)S(1)} %get-tuple-element.66), channel_id=1, source_target_pairs={{0,3},{1,2},{2,1},{3,0},{4,7},{5,6},{6,5},{7,4},{8,11},{9,10},{10,... | collective-permute-start | bytes 202760 | tf_op jit(solution)/shard_map/ppermute | solution.py:37
  31.3 11.4 %collective-permute-start.7 = (bf16[24,2048]{1,0:T(8,128)(2,1)S(1)}, bf16[24,2048]{1,0:T(8,128)(2,1)S(1)}, u32[]{:S(2)}, u32[]{:S(2)}) collective-permute-start(bf16[24,2048]{1,0:T(8,128)(2,1)S(1)} %get-tuple-element.82), channel_id=1, source_target_pairs={{0,1},{1,0},{2,3},{3,2},{4,5},{5,4},{6,7},{7,6},{8,9},{9,8},{10,11... | collective-permute-start | bytes 294920 | tf_op jit(solution)/shard_map/ppermute | solution.py:37
  38.7 6.8 %collective-permute-start.9 = (bf16[24,2048]{1,0:T(8,128)(2,1)S(1)}, bf16[24,2048]{1,0:T(8,128)(2,1)S(1)}, u32[]{:S(2)}, u32[]{:S(2)}) collective-permute-start(bf16[24,2048]{1,0:T(8,128)(2,1)S(1)} %shard_map.153), channel_id=1, source_target_pairs={{0,2},{1,3},{2,0},{3,1},{4,6},{5,7},{6,4},{7,5},{8,10},{9,11},{10,... | collective-permute-start | bytes 294920 | tf_op jit(solution)/shard_map/ppermute | solution.py:37
  42.7 6.5 %collective-permute-start.11 = (bf16[24,2048]{1,0:T(8,128)(2,1)S(1)}, bf16[24,2048]{1,0:T(8,128)(2,1)S(1)}, u32[]{:S(2)}, u32[]{:S(2)}) collective-permute-start(bf16[24,2048]{1,0:T(8,128)(2,1)S(1)} %shard_map.154), channel_id=1, source_target_pairs={{0,3},{1,2},{2,1},{3,0},{4,7},{5,6},{6,5},{7,4},{8,11},{9,10},{10,... | collective-permute-start | bytes 294920 | tf_op jit(solution)/shard_map/ppermute | solution.py:37
  50.9 6.5 %collective-permute-start.22 = (bf16[24,2048]{1,0:T(8,128)(2,1)S(1)}, bf16[24,2048]{1,0:T(8,128)(2,1)S(1)}, u32[]{:S(2)}, u32[]{:S(2)}) collective-permute-start(bf16[24,2048]{1,0:T(8,128)(2,1)S(1)} %get-tuple-element.85.refs_0_), channel_id=1, source_target_pairs={{0,2},{1,3},{2,0},{3,1},{4,6},{5,7},{6,4},{7,5},{8,10},{9,11},{10,... | collective-permute-start | bytes 294920 | tf_op jit(solution)/shard_map/ppermute | solution.py:37
  54.0 6.5 %collective-permute-start.23 = (bf16[24,2048]{1,0:T(8,128)(2,1)S(1)}, bf16[24,2048]{1,0:T(8,128)(2,1)S(1)}, u32[]{:S(2)}, u32[]{:S(2)}) collective-permute-start(bf16[24,2048]{1,0:T(8,128)(2,1)S(1)} %get-tuple-element.85.refs_0_), channel_id=1, source_target_pairs={{0,3},{1,2},{2,1},{3,0},{4,7},{5,6},{6,5},{7,4},{8,11},{9,10},{10,... | collective-permute-start | bytes 294920 | tf_op jit(solution)/shard_map/ppermute | solution.py:37
  60.8 6.0 %collective-permute-start.24 = (bf16[32,2048]{1,0:T(8,128)(2,1)S(1)}, bf16[32,2048]{1,0:T(8,128)(2,1)S(1)}, u32[]{:S(2)}, u32[]{:S(2)}) collective-permute-start(bf16[32,2048]{1,0:T(8,128)(2,1)S(1)} %get-tuple-element.98), channel_id=1, source_target_pairs={{0,4},{4,0},{8,12},{12,8},{1,5},{5,1},{9,13},{13,9},{2,6},{6,2},{1... | collective-permute-start | bytes 393224 | tf_op jit(solution)/shard_map/ppermute | solution.py:37
  62.4 7.0 %collective-permute-start.25 = (bf16[32,2048]{1,0:T(8,128)(2,1)S(1)}, bf16[32,2048]{1,0:T(8,128)(2,1)S(1)}, u32[]{:S(2)}, u32[]{:S(2)}) collective-permute-start(bf16[32,2048]{1,0:T(8,128)(2,1)S(1)} %get-tuple-element.99), channel_id=1, source_target_pairs={{0,8},{4,12},{8,0},{12,4},{1,9},{5,13},{9,1},{13,5},{2,10},{6,14},... | collective-permute-start | bytes 393224 | tf_op jit(solution)/shard_map/ppermute | solution.py:37
  66.9 6.2 %collective-permute-start.26 = (bf16[32,2048]{1,0:T(8,128)(2,1)S(1)}, bf16[32,2048]{1,0:T(8,128)(2,1)S(1)}, u32[]{:S(2)}, u32[]{:S(2)}) collective-permute-start(bf16[32,2048]{1,0:T(8,128)(2,1)S(1)} %get-tuple-element.100), channel_id=1, source_target_pairs={{0,12},{4,8},{8,4},{12,0},{1,13},{5,9},{9,5},{13,1},{2,14},{6,10},... | collective-permute-start | bytes 393224 | tf_op jit(solution)/shard_map/ppermute | solution.py:37
  69.4 11.3 %collective-permute-start.13 = (bf16[24,2048]{1,0:T(8,128)(2,1)S(1)}, bf16[24,2048]{1,0:T(8,128)(2,1)S(1)}, u32[]{:S(2)}, u32[]{:S(2)}) collective-permute-start(bf16[24,2048]{1,0:T(8,128)(2,1)S(1)} %get-tuple-element.89), channel_id=1, source_target_pairs={{0,4},{4,0},{8,12},{12,8},{1,5},{5,1},{9,13},{13,9},{2,6},{6,2},{1... | collective-permute-start | bytes 294920 | tf_op jit(solution)/shard_map/ppermute | solution.py:37
  73.1 9.1 %collective-permute-start.14 = (bf16[24,2048]{1,0:T(8,128)(2,1)S(1)}, bf16[24,2048]{1,0:T(8,128)(2,1)S(1)}, u32[]{:S(2)}, u32[]{:S(2)}) collective-permute-start(bf16[24,2048]{1,0:T(8,128)(2,1)S(1)} %get-tuple-element.90), channel_id=1, source_target_pairs={{0,8},{4,12},{8,0},{12,4},{1,9},{5,13},{9,1},{13,5},{2,10},{6,14},... | collective-permute-start | bytes 294920 | tf_op jit(solution)/shard_map/ppermute | solution.py:37
  74.7 7.4 %collective-permute-start.15 = (bf16[24,2048]{1,0:T(8,128)(2,1)S(1)}, bf16[24,2048]{1,0:T(8,128)(2,1)S(1)}, u32[]{:S(2)}, u32[]{:S(2)}) collective-permute-start(bf16[24,2048]{1,0:T(8,128)(2,1)S(1)} %get-tuple-element.91), channel_id=1, source_target_pairs={{0,12},{4,8},{8,4},{12,0},{1,13},{5,9},{9,5},{13,1},{2,14},{6,10},... | collective-permute-start | bytes 294920 | tf_op jit(solution)/shard_map/ppermute | solution.py:37
  78.6 7.6 %collective-permute-start.27 = (bf16[32,2048]{1,0:T(8,128)(2,1)S(1)}, bf16[32,2048]{1,0:T(8,128)(2,1)S(1)}, u32[]{:S(2)}, u32[]{:S(2)}) collective-permute-start(bf16[32,2048]{1,0:T(8,128)(2,1)S(1)} %get-tuple-element.102), channel_id=1, source_target_pairs={{0,4},{4,0},{8,12},{12,8},{1,5},{5,1},{9,13},{13,9},{2,6},{6,2},{1... | collective-permute-start | bytes 393224 | tf_op jit(solution)/shard_map/ppermute | solution.py:37
  79.2 8.3 %collective-permute-start.28 = (bf16[32,2048]{1,0:T(8,128)(2,1)S(1)}, bf16[32,2048]{1,0:T(8,128)(2,1)S(1)}, u32[]{:S(2)}, u32[]{:S(2)}) collective-permute-start(bf16[32,2048]{1,0:T(8,128)(2,1)S(1)} %get-tuple-element.103), channel_id=1, source_target_pairs={{0,8},{4,12},{8,0},{12,4},{1,9},{5,13},{9,1},{13,5},{2,10},{6,14},... | collective-permute-start | bytes 393224 | tf_op jit(solution)/shard_map/ppermute | solution.py:37
  80.7 6.8 %collective-permute-start.29 = (bf16[32,2048]{1,0:T(8,128)(2,1)S(1)}, bf16[32,2048]{1,0:T(8,128)(2,1)S(1)}, u32[]{:S(2)}, u32[]{:S(2)}) collective-permute-start(bf16[32,2048]{1,0:T(8,128)(2,1)S(1)} %get-tuple-element.104), channel_id=1, source_target_pairs={{0,12},{4,8},{8,4},{12,0},{1,13},{5,9},{9,5},{13,1},{2,14},{6,10},... | collective-permute-start | bytes 393224 | tf_op jit(solution)/shard_map/ppermute | solution.py:37
  87.7 8.9 %collective-permute-start.31 = (bf16[24,2048]{1,0:T(8,128)(2,1)S(1)}, bf16[24,2048]{1,0:T(8,128)(2,1)S(1)}, u32[]{:S(2)}, u32[]{:S(2)}) collective-permute-start(bf16[24,2048]{1,0:T(8,128)(2,1)S(1)} %get-tuple-element.105.refs_10_), channel_id=1, source_target_pairs={{0,2},{1,3},{2,0},{3,1},{4,6},{5,7},{6,4},{7,5},{8,10},{9,11},{10,... | collective-permute-start | bytes 294920 | tf_op jit(solution)/shard_map/ppermute | solution.py:37
  92.1 6.5 %collective-permute-start.32 = (bf16[24,2048]{1,0:T(8,128)(2,1)S(1)}, bf16[24,2048]{1,0:T(8,128)(2,1)S(1)}, u32[]{:S(2)}, u32[]{:S(2)}) collective-permute-start(bf16[24,2048]{1,0:T(8,128)(2,1)S(1)} %get-tuple-element.108), channel_id=1, source_target_pairs={{0,3},{1,2},{2,1},{3,0},{4,7},{5,6},{6,5},{7,4},{8,11},{9,10},{10,... | collective-permute-start | bytes 294920 | tf_op jit(solution)/shard_map/ppermute | solution.py:37
  (21 other events, 203.2 us)
